TPU v7x, 512 devices: a whole 4x4x16 slice. The times are simulated.
512 devices in a mesh: expert: 16 (over z), shard: 32 (over y, x, core).
Axes of the slice: x: 4, y: 4, z: 16, core: 2. Of those that a mesh axis runs over, the one named last changes fastest.
Arguments:
- tokens: bfloat16 [384, 6144], P('expert', 'shard'), may hold values from -6 to 6
- routes: int32 [384, 2], P('expert'), may hold values from 0 to 7, all different within a row; in each aligned block of 24 rows (0 to 23, 24 to 47, ...) at most 12 rows name the same one
- w_router: bfloat16 [6144, 8], replicated, may hold values from -0.078125 to 0.078125
- w_gate: bfloat16 [6144, 65536], P(None, ('expert', 'shard')), may hold values from -0.078125 to 0.078125
- w_up: bfloat16 [6144, 65536], P(None, ('expert', 'shard')), may hold values from -0.078125 to 0.078125
- w_down: bfloat16 [65536, 6144], P(('expert', 'shard')), may hold values from -0.25 to 0.25
Outputs:
- mixed: bfloat16 [384, 6144], P('expert', 'shard')
Inputs may be any that keep to these rules, and one draw needn't show every extreme that they name: `routes`: the two experts of a row differ; within each aligned block of 24 rows no expert is named more than 24 / 2 times, and some expert is named exactly that often.
All inputs are finite; a program needn't handle non-finite values.
Results may differ from a plain program's by a relative error of at most 0.017.
Values may be sent and summed in bfloat16 or wider, within the bound.
No kernel may reach another device: no remote copies, remote signals or barrier semaphores. Data moves between devices by JAX's collectives and lax.ppermute only.
A program may use at most 128 MiB of HBM per device.

v0:
```python
import jax
import jax.numpy as jnp
from jax import lax
from jax.sharding import PartitionSpec as P

FF_W = 8192


def sent_to_all(value, axis):
    peers = lax.axis_size(axis)
    return lax.all_to_all(
        jnp.broadcast_to(value[None], (peers, *value.shape)), axis, 0, 0, tiled=True
    )


def of_everyone(value, axis):
    everything = sent_to_all(value, axis)
    return jnp.sum(everything, axis=0)


def joined_along(blocks, dim):
    blocks = jnp.moveaxis(blocks, 0, dim)
    dims = blocks.shape
    return blocks.reshape(*dims[:dim], dims[dim] * dims[dim + 1], *dims[dim + 2 :])


def gather_directly(value, axis, dim):
    return joined_along(sent_to_all(value, axis), dim)


def cut_along(value, dim, peers):
    before, after = (value.shape[:dim], value.shape[dim + 1 :])
    return jnp.moveaxis(value.reshape(*before, peers, -1, *after), dim, 0)


def sum_at_owner(value, axis, dim):
    blocks = cut_along(value, dim, lax.axis_size(axis))
    arrived = lax.all_to_all(blocks, axis, split_axis=0, concat_axis=0, tiled=True)
    return arrived.astype(jnp.float32).sum(axis=0)


def local(tokens, routes, w_router, w_gate, w_up, w_down):
    tok_dev, dpiece = tokens.shape
    experts = w_router.shape[1]
    capacity = tok_dev // 2
    groups = lax.axis_size("expert")
    shards = lax.axis_size("shard")
    repeat = max(1, groups // experts)
    per_group = max(1, experts // groups)
    width = w_gate.shape[1]
    group_idx = lax.axis_index("expert")
    shard_idx = lax.axis_index("shard")
    expert_here = (group_idx * shards + shard_idx) * width // FF_W
    local_k = expert_here % per_group
    flat = routes.reshape(-1)
    onehot = (flat[:, None] == jnp.arange(experts)[None, :]).astype(jnp.int32)
    rank = jnp.cumsum(onehot, axis=0) - onehot
    slot = jnp.sum(rank * onehot, axis=1)
    target = flat * capacity + slot
    place = (target[:, None] == jnp.arange(experts * capacity)[None, :]).reshape(
        tok_dev, 2, experts * capacity
    )
    dispatch = jnp.any(place, axis=1).T.astype(jnp.bfloat16)
    rows_total = groups * capacity
    router_piece = lax.dynamic_slice_in_dim(w_router, shard_idx * dpiece, dpiece, 0)
    logits = of_everyone(jnp.dot(tokens, router_piece, preferred_element_type=jnp.float32), "shard")
    bucket = jnp.dot(dispatch, tokens, preferred_element_type=jnp.float32).astype(jnp.bfloat16)
    spread = jnp.repeat(bucket.reshape(experts, capacity, -1), repeat, axis=0)
    arrived = lax.all_to_all(
        spread.reshape(groups, per_group, capacity, -1),
        "expert",
        split_axis=0,
        concat_axis=0,
        tiled=True,
    )
    piece = gather_directly(arrived, "shard", 3)
    count = piece.shape[3]
    chosen = lax.dynamic_index_in_dim(piece, local_k, 1, keepdims=False).reshape(rows_total, count)
    gate = jnp.dot(chosen, w_gate, preferred_element_type=jnp.float32)
    up = jnp.dot(chosen, w_up, preferred_element_type=jnp.float32)
    hidden = (jax.nn.silu(gate) * up).astype(jnp.bfloat16)
    partial_out = jnp.dot(hidden, w_down, preferred_element_type=jnp.float32)
    keep = jnp.arange(per_group) == local_k
    term = jnp.where(keep[None, :, None, None], partial_out.reshape(groups, 1, capacity, -1), 0.0)
    shares = sum_at_owner(term.astype(jnp.bfloat16), "shard", 3)
    back = lax.all_to_all(
        shares.astype(jnp.bfloat16), "expert", split_axis=0, concat_axis=0, tiled=True
    )
    expert_out = jnp.sum(
        back.astype(jnp.float32).reshape(experts, repeat, capacity, dpiece), axis=1
    )
    expert_out = expert_out.reshape(experts * capacity, dpiece)
    picks = jnp.sum(
        jnp.where(
            routes[:, :, None] == jnp.arange(experts)[None, None, :], logits[:, None, :], 0.0
        ),
        axis=2,
    )
    first = 1.0 / (1.0 + jnp.exp(picks[:, 1] - picks[:, 0]))
    second = 1.0 / (1.0 + jnp.exp(picks[:, 0] - picks[:, 1]))
    weights = jnp.stack([first, second], axis=1)
    combine = jnp.sum(jnp.where(place, weights[:, :, None], 0.0), axis=1)
    mixed = jnp.dot(
        combine, expert_out, precision=lax.Precision.HIGHEST, preferred_element_type=jnp.float32
    )
    return mixed.astype(jnp.bfloat16)


def solution(mesh):
    return jax.shard_map(
        local,
        mesh=mesh,
        in_specs=(
            P("expert", "shard"),
            P("expert", None),
            P(),
            P(None, ("expert", "shard")),
            P(None, ("expert", "shard")),
            P(("expert", "shard"), None),
        ),
        out_specs=P("expert", "shard"),
        check_vma=False,
    )
```

profile of v0, /device:TPU:1, one launch (start us, length us, event | category | flops | bytes accessed | tf_op | source)
XLA Modules:
  0.0 186.6 jit_solution(6360991764029700150)
XLA Ops:
  0.0 0.0 copy-start
  0.0 0.9 copy.51
  0.9 0.1 eq.23
  1.0 0.1 fusion.8
  1.1 0.1 reduce_window_sum.11
  1.1 0.2 select_reduce_fusion.1
  1.3 0.1 reduce_sum.62
  1.4 0.1 copy.52
  1.5 0.7 multiply_add_fusion
  2.2 0.1 fusion.7
  2.3 0.9 convolution_convert_fusion.1
  3.2 27.5 %all_to_all.25 = bf16[16,1,12,192]{3,2,1,0:T(8,128)(2,1)S(1)} all-to-all(bf16[16,1,12,192]{3,2,1,0:T(8,128)(2,1)S(1)} %bitcast.34), channel_id=1, replica_groups=mesh['expert'=16,'shard'=32] {'expert'}, dimensions={0} | all-to-all | bytes 147456 | tf_op jit(solution)/shard_map/all_to_all | solution.py:69
  30.8 2.1 %broadcast_in_dim.64 = bf16[32,16,1,12,192]{4,1,3,2,0:T(8,128)(2,1)} broadcast(bf16[16,12,192]{2,0,1:T(8,128)(2,1)S(1)} %copy.53), dimensions={1,3,4} | broadcast | bytes 2433024 | tf_op jit(solution)/shard_map/broadcast_in_dim | solution.py:12
  32.9 0.0 copy-start.2
  32.9 10.9 %all-to-all-start.2 = ((bf16[32,16,1,12,192]{4,1,3,2,0:T(8,128)(2,1)}), bf16[32,16,1,12,192]{4,1,3,2,0:T(8,128)(2,1)}, u32[]{:S(2)}, u32[]{:S(2)}) async-start(bf16[32,16,1,12,192]{4,1,3,2,0:T(8,128)(2,1)} %broadcast_in_dim.64), calls=%async_computation.2 | async-start | bytes 6291456 | tf_op jit(solution)/shard_map/all_to_all | solution.py:11
  43.8 0.0 copy-done.2
  43.8 0.9 convolution_bitcast_fusion
  44.7 0.7 reshape.73
  45.5 37.6 %all-to-all-done.2 = bf16[32,16,1,12,192]{4,1,3,2,0:T(8,128)(2,1)} async-done(((bf16[32,16,1,12,192]{4,1,3,2,0:T(8,128)(2,1)}), bf16[32,16,1,12,192]{4,1,3,2,0:T(8,128)(2,1)}, u32[]{:S(2)}, u32[]{:S(2)}) %all-to-all-start.2) | async-done | bytes 2359328 | tf_op jit(solution)/shard_map/all_to_all | solution.py:11
  83.0 6.3 %all-to-all-start = ((f32[32,1,192]{2,1,0:T(1,128)}), f32[32,1,192]{2,1,0:T(1,128)S(1)}, u32[]{:S(2)}, u32[]{:S(2)}) async-start(f32[32,1,192]{2,1,0:T(1,128)} %reshape.73), calls=%async_computation | async-start | bytes 65536 | tf_op jit(solution)/shard_map/all_to_all | solution.py:11
  89.3 5.4 %copy.54 = bf16[16,1,12,32,192]{4,3,2,0,1:T(8,128)(2,1)} copy(bf16[16,1,12,32,192]{4,0,2,1,3:T(8,128)(2,1)} %bitcast.3) | data formatting | bytes 4718592 | tf_op jit(solution)/shard_map/transpose | solution.py:22
  94.7 0.0 copy-start.1
  94.7 6.3 %reshape.67 = bf16[192,6144]{1,0:T(8,128)(2,1)} reshape(bf16[16,1,12,32,192]{4,3,2,0,1:T(8,128)(2,1)} %copy.54) | data formatting | bytes 4718592 | tf_op jit(solution)/shard_map/reshape | solution.py:78
  101.0 0.0 copy-done.1
  101.0 2.4 %fusion.12 = f32[192,128]{1,0:T(8,128)S(1)} fusion(bf16[192,6144]{1,0:T(8,128)(2,1)} %reshape.67, bf16[6144,128]{1,0:T(8,128)(2,1)S(1)} %copy-done.1), kind=kOutput, calls=%fused_computation.31 | convolution fusion | flops 301989888 | bytes 4030464 | tf_op jit(solution)/shard_map/dot_general | solution.py:79
  103.4 0.0 copy-done
  103.4 5.0 %convolution_convert_fusion = bf16[192,6144]{1,0:T(8,128)(2,1)} fusion(bf16[128,6144]{1,0:T(8,128)(2,1)S(1)} %copy-done, bf16[192,6144]{1,0:T(8,128)(2,1)} %reshape.67, bf16[6144,128]{1,0:T(8,128)(2,1)} %param.10, f32[192,128]{1,0:T(8,128)S(1)} %fusion.12), kind=kOutput, calls=%fused_computation | convolution fusion | flops 605306880 | bytes 7962624 | tf_op jit(solution)/shard_map/dot_general | solution.py:82
  108.4 6.4 %convert_element_type.35 = bf16[16,1,12,32,192]{4,3,2,0,1:T(8,128)(2,1)} reshape(bf16[192,6144]{1,0:T(8,128)(2,1)} %convolution_convert_fusion) | data formatting | bytes 4718592 | tf_op jit(solution)/shard_map/convert_element_type | solution.py:85
  114.9 5.3 %copy.58 = bf16[16,1,12,32,192]{4,0,2,1,3:T(8,128)(2,1)} copy(bf16[16,1,12,32,192]{4,3,2,0,1:T(8,128)(2,1)} %convert_element_type.35) | data formatting | bytes 4718592 | tf_op jit(solution)/shard_map/convert_element_type | solution.py:85
  120.2 0.0 all-to-all-done
  120.2 0.0 copy-start.3
  120.2 7.7 %all-to-all-start.3 = ((bf16[32,16,1,12,192]{4,1,3,2,0:T(8,128)(2,1)}), bf16[32,16,1,12,192]{4,1,3,2,0:T(8,128)(2,1)}, u32[]{:S(2)}, u32[]{:S(2)}) async-start(bf16[32,16,1,12,192]{4,1,3,2,0:T(8,128)(2,1)} %bitcast.31), calls=%async_computation.3 | async-start | bytes 6291456 | tf_op jit(solution)/shard_map/all_to_all | solution.py:38
  127.9 0.5 broadcast.44
  128.4 0.7 reduce.2
  129.1 0.1 reshape.74
  129.3 0.0 copy-done.3
  129.3 37.8 %all-to-all-done.3 = bf16[32,16,1,12,192]{4,1,3,2,0:T(8,128)(2,1)} async-done(((bf16[32,16,1,12,192]{4,1,3,2,0:T(8,128)(2,1)}), bf16[32,16,1,12,192]{4,1,3,2,0:T(8,128)(2,1)}, u32[]{:S(2)}, u32[]{:S(2)}) %all-to-all-start.3) | async-done | bytes 2359328 | tf_op jit(solution)/shard_map/all_to_all | solution.py:38
  167.1 2.4 %reduce_sum.66 = bf16[16,12,192]{2,0,1:T(8,128)(2,1)S(1)} reduce(bf16[32,16,1,12,192]{4,1,3,2,0:T(8,128)(2,1)} %all-to-all-done.3, bf16[]{:T(256)} %constant.60.clone.1), dimensions={0,2}, to_apply=%region_6.7 | reduce | flops 1142784 | bytes 2433026 | tf_op jit(solution)/shard_map/reduce_sum | solution.py:39
  169.6 0.7 copy.56
  170.2 3.6 %all-to-all-start.4 = ((bf16[16,1,12,192]{3,2,1,0:T(8,128)(2,1)}), bf16[16,1,12,192]{3,2,1,0:T(8,128)(2,1)S(1)}, u32[]{:S(2)}, u32[]{:S(2)}) async-start(bf16[16,1,12,192]{3,2,1,0:T(8,128)(2,1)} %copy.56), calls=%async_computation.4 | async-start | bytes 262144 | tf_op jit(solution)/shard_map/all_to_all | solution.py:86
  173.8 0.1 select_reduce_fusion
  173.9 11.9 %all-to-all-done.4 = bf16[16,1,12,192]{3,2,1,0:T(8,128)(2,1)S(1)} async-done(((bf16[16,1,12,192]{3,2,1,0:T(8,128)(2,1)}), bf16[16,1,12,192]{3,2,1,0:T(8,128)(2,1)S(1)}, u32[]{:S(2)}, u32[]{:S(2)}) %all-to-all-start.4) | async-done | bytes 73760 | tf_op jit(solution)/shard_map/all_to_all | solution.py:86
  185.8 0.8 convolution_convert_fusion.2
  (10 shorter events, 0.2 us)
Async XLA Ops:
  0.0 103.4 %copy-start = (bf16[128,6144]{1,0:T(8,128)(2,1)S(1)}, bf16[128,6144]{1,0:T(8,128)(2,1)}, u32[]{:S(2)}) copy-start(bf16[128,6144]{1,0:T(8,128)(2,1)} %param.11) | copy-start | bytes 4718596
  32.9 10.9 %copy-start.2 = (bf16[24,192]{1,0:T(8,128)(2,1)S(1)}, bf16[24,192]{1,0:T(8,128)(2,1)}, u32[]{:S(2)}) copy-start(bf16[24,192]{1,0:T(8,128)(2,1)} %param.6) | copy-start | bytes 27652
  32.9 50.1 %all-to-all-start.2 = ((bf16[32,16,1,12,192]{4,1,3,2,0:T(8,128)(2,1)}), bf16[32,16,1,12,192]{4,1,3,2,0:T(8,128)(2,1)}, u32[]{:S(2)}, u32[]{:S(2)}) async-start(bf16[32,16,1,12,192]{4,1,3,2,0:T(8,128)(2,1)} %broadcast_in_dim.64), calls=%async_computation.2 | async-start | bytes 6291456 | tf_op jit(solution)/shard_map/all_to_all | solution.py:11
  83.0 37.2 %all-to-all-start = ((f32[32,1,192]{2,1,0:T(1,128)}), f32[32,1,192]{2,1,0:T(1,128)S(1)}, u32[]{:S(2)}, u32[]{:S(2)}) async-start(f32[32,1,192]{2,1,0:T(1,128)} %reshape.73), calls=%async_computation | async-start | bytes 65536 | tf_op jit(solution)/shard_map/all_to_all | solution.py:11
  94.7 6.3 %copy-start.1 = (bf16[6144,128]{1,0:T(8,128)(2,1)S(1)}, bf16[6144,128]{1,0:T(8,128)(2,1)}, u32[]{:S(2)}) copy-start(bf16[6144,128]{1,0:T(8,128)(2,1)} %param.9) | copy-start | bytes 4718596
  120.2 9.1 %copy-start.3 = (s32[24,2]{0,1:T(2,128)S(1)}, s32[24,2]{0,1:T(2,128)}, u32[]{:S(2)}) copy-start(s32[24,2]{0,1:T(2,128)} %param.7) | copy-start | bytes 580
  120.2 46.9 %all-to-all-start.3 = ((bf16[32,16,1,12,192]{4,1,3,2,0:T(8,128)(2,1)}), bf16[32,16,1,12,192]{4,1,3,2,0:T(8,128)(2,1)}, u32[]{:S(2)}, u32[]{:S(2)}) async-start(bf16[32,16,1,12,192]{4,1,3,2,0:T(8,128)(2,1)} %bitcast.31), calls=%async_computation.3 | async-start | bytes 6291456 | tf_op jit(solution)/shard_map/all_to_all | solution.py:38
  170.2 15.5 %all-to-all-start.4 = ((bf16[16,1,12,192]{3,2,1,0:T(8,128)(2,1)}), bf16[16,1,12,192]{3,2,1,0:T(8,128)(2,1)S(1)}, u32[]{:S(2)}, u32[]{:S(2)}) async-start(bf16[16,1,12,192]{3,2,1,0:T(8,128)(2,1)} %copy.56), calls=%async_computation.4 | async-start | bytes 262144 | tf_op jit(solution)/shard_map/all_to_all | solution.py:86
where the time goes:
time: 190 us; the launch traced here: 187 us
  waiting for transfers between devices  87.2 us (46%)
  local copies, waits for them, and re-layouts  28.8 us (15%)
  starting transfers between devices  28.4 us (15%)
  blocking collectives  27.5 us (14%)
  matrix products  10 us (5%)
  other arithmetic  4.44 us (2%)
    all_to_all x1, waiting for transfers between devices, sum_at_owner(): lax.all_to_all(blocks, axis, split_axis=0, concat_axis=0, tiled=True)  37.8 us
    all_to_all x2, waiting for transfers between devices, sent_to_all(): lax.all_to_all(jnp.broadcast_to(value[None], (peers, *value.shape)), axis...  37.6 us
    all_to_all x1, blocking collectives, local(): lax.all_to_all(spread.reshape(groups, per_group, capacity, -1), 'expert',...  27.5 us
    all_to_all x2, starting transfers between devices, sent_to_all(): lax.all_to_all(jnp.broadcast_to(value[None], (peers, *value.shape)), axis...  17.2 us
    all_to_all x1, waiting for transfers between devices, local(): lax.all_to_all(shares.astype(jnp.bfloat16), 'expert', split_axis=0, conca...  11.9 us
    convert_element_type x2, local copies, waits for them, and re-layouts, local(): shares = sum_at_owner(term.astype(jnp.bfloat16), 'shard', 3)  11.8 us
    all_to_all x1, starting transfers between devices, sum_at_owner(): lax.all_to_all(blocks, axis, split_axis=0, concat_axis=0, tiled=True)  7.68 us
    reshape x1, local copies, waits for them, and re-layouts, local(): lax.dynamic_index_in_dim(piece, local_k, 1, keepdims=False)  6.31 us
  transfers between devices with their start and end apart: 4, of which 3 were waited for; matrix products, arithmetic and copies ran while one was open for 18% of the time, Pallas kernels for 0%

commit v1 on v0

v1 whole, which is shorter than its diff:
```python
import jax
import jax.numpy as jnp
from jax import lax
from jax.experimental import pallas as pl
from jax.experimental.pallas import tpu as pltpu
from jax.sharding import Mesh, PartitionSpec as P

EXPERTS = 8
CAP = 12
HALF = 6
PLANES = 16
CHIPS = 16
ROWS = PLANES * HALF
TOK = 24
FEAT = 192
PAIR = 384
D = 6144
PADR = 8
LANES = 256
F32 = jnp.float32
BF16 = jnp.bfloat16
VM = pltpu.VMEM


def vmem():
    return pl.BlockSpec(memory_space=pltpu.VMEM)


def smem():
    return pl.BlockSpec(memory_space=pltpu.SMEM)


def iota(shape, dim):
    return lax.broadcasted_iota(jnp.int32, shape, dim)


def dot_nt(a, b):
    return lax.dot_general(a, b, (((1,), (1,)), ((), ())), preferred_element_type=F32)


def dot_tn(a, b):
    return lax.dot_general(a, b, (((0,), (0,)), ((), ())), preferred_element_type=F32)


def dot_nn(a, b):
    return jnp.dot(a, b, preferred_element_type=F32)


def dispatch_kernel(core_ref, routes_ref, tok_ref, out_ref, place_ref):
    core = core_ref[0]
    total = 2 * PLANES * PADR
    first = routes_ref[0:1, :]
    second = routes_ref[1:2, :]
    k8 = iota((EXPERTS, TOK), 0)
    named = ((k8 == first) | (k8 == second)).astype(F32)
    earlier = (iota((TOK, TOK), 0) < iota((TOK, TOK), 1)).astype(BF16)
    rank = dot_nn(named.astype(BF16), earlier)
    row = iota((total, EXPERTS), 0)
    pick = ((row >> 5) == iota((total, EXPERTS), 1)).astype(BF16)
    named_row = dot_nn(pick, named.astype(BF16))
    rank_row = dot_nn(pick, rank.astype(BF16))
    r = iota((total, TOK), 0)
    slot = (r & 7) + HALF * ((r >> 3) & 1)
    hit = (named_row > 0.5) & (rank_row == slot.astype(F32)) & ((r & 7) < HALF)
    place = hit.astype(F32).astype(BF16)
    place_ref[...] = place
    tok = tok_ref[...].astype(F32)
    wide = jnp.concatenate([tok, jnp.zeros((TOK, LANES - FEAT), F32)], axis=1)
    shifted = jnp.concatenate([jnp.zeros((TOK, LANES - FEAT), F32), tok], axis=1)
    wide = jnp.where(core == 0, wide, shifted).astype(BF16)
    lane = iota((LANES, TOK), 0) - jnp.where(core == 0, FEAT, 0)
    info = ((lane == first) | (lane == second)).astype(F32).astype(BF16)
    payload = dot_nn(place, wide) + dot_nt(place, info)
    out_ref[...] = payload.reshape(2 * PLANES, PADR, LANES).astype(BF16)


def repack_kernel(in_ref, out_ref, info_ref):
    x = in_ref[...].astype(F32).reshape(PLANES, 2, PADR, LANES)
    low = x[:, 0].reshape(PLANES * PADR, LANES).astype(BF16)
    high = x[:, 1].reshape(PLANES * PADR, LANES).astype(BF16)
    p = iota((ROWS, PLANES * PADR), 0)
    home = (p * 43) >> 8
    keep = (iota((ROWS, PLANES * PADR), 1) == p + 2 * home).astype(F32).astype(BF16)
    a = dot_nn(keep, low)
    b = dot_nn(keep, high)
    left = iota((ROWS, 128), 1) < 64
    middle = jnp.where(left, a[:, 128:], b[:, :128])
    block = jnp.concatenate([a[:, :128], middle, b[:, 128:]], axis=1).astype(BF16)
    for chip in range(CHIPS):
        out_ref[chip] = block
    info_ref[...] = a[:, 128:]


def expert_kernel(
    expert_ref, x_ref, info_ref, router_ref, gate_a, gate_b, up_a, up_b, down_a, down_b, out_ref
):
    expert = expert_ref[0]
    gate = jnp.zeros((ROWS, 256), F32)
    up = jnp.zeros((ROWS, 256), F32)
    logits = jnp.zeros((ROWS, EXPERTS), F32)
    for chip in range(CHIPS):
        rows = slice(chip * PAIR, (chip + 1) * PAIR)
        x = x_ref[chip]
        gate = gate + dot_nn(x, jnp.concatenate([gate_a[rows, :], gate_b[rows, :]], axis=1))
        up = up + dot_nn(x, jnp.concatenate([up_a[rows, :], up_b[rows, :]], axis=1))
        logits = logits + dot_nt(x, router_ref[:, rows])
    k = iota((ROWS, EXPERTS), 1)
    named = info_ref[:, 64 : 64 + EXPERTS]
    other = jnp.sum(jnp.where((k != expert) & (named > 0.5), logits, 0.0), axis=1, keepdims=True)
    own = jnp.sum(jnp.where(k == expert, logits, 0.0), axis=1, keepdims=True)
    weight = 1.0 / (1.0 + jnp.exp(other - own))
    hidden = (gate / (1.0 + jnp.exp(-gate)) * up * weight).astype(BF16)
    for chip in range(CHIPS):
        cols = slice(chip * PAIR, (chip + 1) * PAIR)
        down = jnp.concatenate([down_a[:, cols], down_b[:, cols]], axis=0)
        out_ref[chip] = dot_nn(hidden, down).astype(BF16)


def share_kernel(in_ref, out_ref):
    total = in_ref[0].astype(F32)
    for chip in range(1, CHIPS):
        total = total + in_ref[chip].astype(F32)
    total = total.astype(BF16)
    p = iota((PLANES * PADR, ROWS), 1)
    home = (p * 43) >> 8
    put = (iota((PLANES * PADR, ROWS), 0) == p + 2 * home).astype(F32).astype(BF16)
    spread = dot_nn(put, total).reshape(PLANES, PADR, PAIR)
    low = spread[:, :, :256].reshape(PLANES, 1, PADR, LANES)
    high = spread[:, :, 128:].reshape(PLANES, 1, PADR, LANES)
    both = jnp.concatenate([low, high], axis=1)
    out_ref[...] = both.reshape(2 * PLANES, PADR, LANES).astype(BF16)


def combine_kernel(core_ref, place_ref, in_ref, out_ref):
    core = core_ref[0]
    x = in_ref[...].astype(F32).reshape(2 * PLANES * PADR, LANES).astype(BF16)
    mixed = dot_tn(place_ref[...], x)
    out_ref[...] = jnp.where(core == 0, mixed[:, :FEAT], mixed[:, LANES - FEAT :]).astype(BF16)


def local(tokens, routes, w_router, w_gate, w_up, w_down):
    core = lax.axis_index("c").reshape(1).astype(jnp.int32)
    expert = (lax.axis_index("z") // (PLANES // EXPERTS)).reshape(1).astype(jnp.int32)
    swap = [(0, 1), (1, 0)]
    gate_b = lax.ppermute(w_gate, "c", swap)
    up_b = lax.ppermute(w_up, "c", swap)
    down_b = lax.ppermute(w_down, "c", swap)
    payload, place = pl.pallas_call(
        dispatch_kernel,
        out_shape=(
            jax.ShapeDtypeStruct((2 * PLANES, PADR, LANES), BF16),
            jax.ShapeDtypeStruct((2 * PLANES * PADR, TOK), BF16),
        ),
        in_specs=[smem(), vmem(), vmem()],
        out_specs=(vmem(), vmem()),
        name="dispatch",
    )(core, routes.T, tokens)
    arrived = lax.all_to_all(payload, ("z", "c"), 0, 0, tiled=True)
    blocks, info = pl.pallas_call(
        repack_kernel,
        out_shape=(
            jax.ShapeDtypeStruct((CHIPS, ROWS, PAIR), BF16),
            jax.ShapeDtypeStruct((ROWS, 128), F32),
        ),
        in_specs=[vmem()],
        out_specs=(vmem(), vmem()),
        name="repack",
    )(arrived)
    gathered = lax.all_to_all(blocks, ("y", "x"), 0, 0, tiled=True)
    terms = pl.pallas_call(
        expert_kernel,
        out_shape=jax.ShapeDtypeStruct((CHIPS, ROWS, PAIR), BF16),
        in_specs=[smem()] + [vmem()] * 9,
        out_specs=vmem(),
        compiler_params=pltpu.CompilerParams(vmem_limit_bytes=24 << 20),
        name="expert",
    )(expert, gathered, info, w_router.T, w_gate, gate_b, w_up, up_b, w_down, down_b)
    parts = lax.all_to_all(terms, ("y", "x"), 0, 0, tiled=True)
    shares = pl.pallas_call(
        share_kernel,
        out_shape=jax.ShapeDtypeStruct((2 * PLANES, PADR, LANES), BF16),
        in_specs=[vmem()],
        out_specs=vmem(),
        name="share",
    )(parts)
    back = lax.all_to_all(shares, ("z", "c"), 0, 0, tiled=True)
    return pl.pallas_call(
        combine_kernel,
        out_shape=jax.ShapeDtypeStruct((TOK, FEAT), BF16),
        in_specs=[smem(), vmem(), vmem()],
        out_specs=vmem(),
        name="combine",
    )(core, place, back)


def solution(mesh):
    fine = Mesh(mesh.devices.reshape(16, 4, 4, 2), ("z", "y", "x", "c"))
    shard = ("y", "x", "c")
    both = ("z",) + shard
    return jax.shard_map(
        local,
        mesh=fine,
        in_specs=(P("z", shard), P("z", None), P(), P(None, both), P(None, both), P(both, None)),
        out_specs=P("z", shard),
        check_vma=False,
    )
```

time: 190 us -> 120 us (0.63); the launches traced: 187 us -> 119 us
  waiting for transfers between devices: 87.2 us -> 25.8 us
  local copies, waits for them, and re-layouts: 28.8 us -> 3.48 us
  blocking collectives: 27.5 us -> 47 us
  Pallas kernels: 0 us -> 13 us
  matrix products: 10 us -> 0 us
  other arithmetic: 4.44 us -> 0 us
    all_to_all x4 -> x2, waiting for transfers between devices: 87.2 us -> 25.8 us  [the longest x1 16.4 us: local(): gathered = lax.all_to_all(blocks, ('y', 'x'), 0, 0, tiled=True)]
    all_to_all x1 -> x2, blocking collectives: 27.5 us -> 47 us  [the longest x1 25.1 us: local(): back = lax.all_to_all(shares, ('z', 'c'), 0, 0, tiled=True)]
    pallas_call x0 -> x5, Pallas kernels: none -> 13 us  [the longest x1 4.73 us: local(): pl.pallas_call(expert_kernel, out_shape=jax.ShapeDtypeStruct((CHIPS, ROWS...]
    convert_element_type x2 -> x0, local copies, waits for them, and re-layouts: 11.8 us -> none  [local(): shares = sum_at_owner(term.astype(jnp.bfloat16), 'shard', 3)]
    dot_general x5 -> x0, matrix products: 10 us -> none  [the longest x1 5.01 us: local(): partial_out = jnp.dot(hidden, w_down, preferred_element_type=jnp.float32)]
    ppermute x0 -> x3, starting transfers between devices: none -> 6.48 us  [the longest x1 2.19 us: local(): up_b = lax.ppermute(w_up, 'c', swap)]
    reshape x3 -> x0, local copies, waits for them, and re-layouts: 6.34 us -> none  [the longest x1 6.31 us: local(): lax.dynamic_index_in_dim(piece, local_k, 1, keepdims=False)]
    transpose x1 -> x0, local copies, waits for them, and re-layouts: 5.36 us -> none  [joined_along(): blocks = jnp.moveaxis(blocks, 0, dim)]
  transfers between devices with their start and end apart: 4 -> 5, of which waited for: 3 -> 2; matrix products, arithmetic and copies ran while one was open for 18% -> 0% of each run, Pallas kernels for 0% -> 2%
where the time goes in v1:
time: 120 us; the launch traced here: 119 us
  blocking collectives  47 us (39%)
  starting transfers between devices  30.1 us (25%)
  waiting for transfers between devices  25.8 us (22%)
  Pallas kernels  13 us (11%)
  local copies, waits for them, and re-layouts  3.48 us (3%)
    all_to_all x1, blocking collectives, local(): back = lax.all_to_all(shares, ('z', 'c'), 0, 0, tiled=True)  25.1 us
    all_to_all x1, blocking collectives, local(): parts = lax.all_to_all(terms, ('y', 'x'), 0, 0, tiled=True)  22 us
    all_to_all x1, starting transfers between devices, local(): arrived = lax.all_to_all(payload, ('z', 'c'), 0, 0, tiled=True)  16.8 us
    all_to_all x1, waiting for transfers between devices, local(): gathered = lax.all_to_all(blocks, ('y', 'x'), 0, 0, tiled=True)  16.4 us
    all_to_all x1, waiting for transfers between devices, local(): arrived = lax.all_to_all(payload, ('z', 'c'), 0, 0, tiled=True)  9.34 us
    all_to_all x1, starting transfers between devices, local(): gathered = lax.all_to_all(blocks, ('y', 'x'), 0, 0, tiled=True)  6.88 us
    pallas_call x1, Pallas kernels, local(): pl.pallas_call(expert_kernel, out_shape=jax.ShapeDtypeStruct((CHIPS, ROWS...  4.73 us
    unnamed x12, local copies, waits for them, and re-layouts  3.48 us
  transfers between devices with their start and end apart: 5, of which 2 were waited for; matrix products, arithmetic and copies ran while one was open for 0% of the time, Pallas kernels for 2%

profile of v1, /device:TPU:1, one launch (start us, length us, event | category | flops | bytes accessed | tf_op | source)
XLA Modules:
  0.0 119.5 jit_solution(13434473713831411501)
XLA Ops:
  0.0 0.0 copy-start
  0.0 0.0 copy-start.3
  0.0 2.0 %dispatch.1 = (bf16[32,8,256]{2,1,0:T(8,128)(2,1)}, bf16[256,24]{1,0:T(8,128)(2,1)}) custom-call(s32[1]{0:T(128)} %bitcast.core_ref, s32[2,24]{1,0:T(2,128)} %bitcast.5, bf16[24,192]{1,0:T(8,128)(2,1)} %tok_ref.1), custom_call_target="tpu_custom_call" | custom-call | tf_op jit(solution)/shard_map/dispatch/pallas_call | solution.py:148
  2.0 16.8 %all-to-all-start = ((bf16[32,8,256]{2,1,0:T(8,128)(2,1)}), bf16[32,8,256]{2,1,0:T(8,128)(2,1)S(1)}, u32[]{:S(2)}, u32[]{:S(2)}) async-start(bf16[32,8,256]{2,1,0:T(8,128)(2,1)} %get-tuple-element.10), calls=%async_computation | async-start | bytes 262144 | tf_op jit(solution)/shard_map/all_to_all | solution.py:158
  18.8 2.1 %collective-permute-start = (bf16[6144,128]{1,0:T(8,128)(2,1)}, bf16[6144,128]{1,0:T(8,128)(2,1)}, u32[]{:S(2)}, u32[]{:S(2)}) collective-permute-start(bf16[6144,128]{1,0:T(8,128)(2,1)} %gate_a.1), channel_id=1, source_target_pairs={{0,1},{1,0},{2,3},{3,2},{4,5},{5,4},{6,7},{7,6},{8,9},{9,8},{10,11... | collective-permute-start | bytes 4718600 | tf_op jit(solution)/shard_map/ppermute | solution.py:145
  20.9 2.2 %collective-permute-start.1 = (bf16[6144,128]{1,0:T(8,128)(2,1)}, bf16[6144,128]{1,0:T(8,128)(2,1)}, u32[]{:S(2)}, u32[]{:S(2)}) collective-permute-start(bf16[6144,128]{1,0:T(8,128)(2,1)} %up_a.1), channel_id=1, source_target_pairs={{0,1},{1,0},{2,3},{3,2},{4,5},{5,4},{6,7},{7,6},{8,9},{9,8},{10,11... | collective-permute-start | bytes 4718600 | tf_op jit(solution)/shard_map/ppermute | solution.py:146
  23.1 2.1 %collective-permute-start.2 = (bf16[128,6144]{1,0:T(8,128)(2,1)}, bf16[128,6144]{1,0:T(8,128)(2,1)}, u32[]{:S(2)}, u32[]{:S(2)}) collective-permute-start(bf16[128,6144]{1,0:T(8,128)(2,1)} %down_a.1), channel_id=1, source_target_pairs={{0,1},{1,0},{2,3},{3,2},{4,5},{5,4},{6,7},{7,6},{8,9},{9,8},{10,11... | collective-permute-start | bytes 4718600 | tf_op jit(solution)/shard_map/ppermute | solution.py:147
  25.3 9.3 %all-to-all-done.in_ref = bf16[32,8,256]{2,1,0:T(8,128)(2,1)S(1)} async-done(((bf16[32,8,256]{2,1,0:T(8,128)(2,1)}), bf16[32,8,256]{2,1,0:T(8,128)(2,1)S(1)}, u32[]{:S(2)}, u32[]{:S(2)}) %all-to-all-start) | async-done | bytes 131104 | tf_op jit(solution)/shard_map/all_to_all | solution.py:158
  34.6 0.0 copy-start.5
  34.6 0.7 copy-done.5
  35.3 2.2 %repack.1 = (bf16[16,96,384]{2,1,0:T(8,128)(2,1)}, f32[96,128]{1,0:T(8,128)}) custom-call(bf16[32,8,256]{2,1,0:T(8,128)(2,1)} %copy-done.5), custom_call_target="tpu_custom_call" | custom-call | tf_op jit(solution)/shard_map/repack/pallas_call | solution.py:159
  37.5 0.0 copy-start.4
  37.5 6.9 %all-to-all-start.1 = ((bf16[16,96,384]{2,1,0:T(8,128)(2,1)}), bf16[16,96,384]{2,1,0:T(8,128)(2,1)S(1)}, u32[]{:S(2)}, u32[]{:S(2)}) async-start(bf16[16,96,384]{2,1,0:T(8,128)(2,1)} %get-tuple-element.11), calls=%async_computation.1 | async-start | bytes 2359296 | tf_op jit(solution)/shard_map/all_to_all | solution.py:169
  44.4 0.0 collective-permute-done.gate_b
  44.4 0.0 collective-permute-done.1.up_b
  44.4 0.0 collective-permute-done.2.down_b
  44.4 16.4 %all-to-all-done.1.x_ref = bf16[16,96,384]{2,1,0:T(8,128)(2,1)S(1)} async-done(((bf16[16,96,384]{2,1,0:T(8,128)(2,1)}), bf16[16,96,384]{2,1,0:T(8,128)(2,1)S(1)}, u32[]{:S(2)}, u32[]{:S(2)}) %all-to-all-start.1) | async-done | bytes 1179680 | tf_op jit(solution)/shard_map/all_to_all | solution.py:169
  60.8 0.0 copy-done
  60.8 0.0 copy-done.3
  60.8 0.0 copy-done.4
  60.8 0.0 copy-start.1
  60.9 1.4 %copy-done.1 = bf16[6144,128]{1,0:T(8,128)(2,1)S(1)} copy-done((bf16[6144,128]{1,0:T(8,128)(2,1)S(1)}, bf16[6144,128]{1,0:T(8,128)(2,1)}, u32[]{:S(2)}) %copy-start.1) | copy-done | bytes 1572888
  62.3 0.0 copy-start.2
  62.3 1.4 %copy-done.2 = bf16[128,6144]{1,0:T(8,128)(2,1)S(1)} copy-done((bf16[128,6144]{1,0:T(8,128)(2,1)S(1)}, bf16[128,6144]{1,0:T(8,128)(2,1)}, u32[]{:S(2)}) %copy-start.2) | copy-done | bytes 1572888
  63.7 4.7 %expert.1 = bf16[16,96,384]{2,1,0:T(8,128)(2,1)S(1)} custom-call(s32[1]{0:T(128)} %bitcast.2.expert_ref, bf16[16,96,384]{2,1,0:T(8,128)(2,1)S(1)} %all-to-all-done.1.x_ref, f32[96,128]{1,0:T(8,128)S(1)} %copy-done.4, bf16[8,6144]{1,0:T(8,128)(2,1)S(1)} %bitcast.4, bf16[6144,128]{1,0:T(8,128)(2,1)S(1)} %copy-done, ...), custom_call_target="tpu_custom_call" | custom-call | tf_op jit(solution)/shard_map/expert/pallas_call | solution.py:170
  68.4 22.0 %all_to_all.20.in_ref = bf16[16,96,384]{2,1,0:T(8,128)(2,1)} all-to-all(bf16[16,96,384]{2,1,0:T(8,128)(2,1)S(1)} %expert.1), channel_id=1, replica_groups=mesh['z'=16,'y'=4,'x'=4,'c'=2] {'y','x'}, dimensions={0} | all-to-all | bytes 2359296 | tf_op jit(solution)/shard_map/all_to_all | solution.py:178
  90.4 2.2 %share.1 = bf16[32,8,256]{2,1,0:T(8,128)(2,1)} custom-call(bf16[16,96,384]{2,1,0:T(8,128)(2,1)} %all_to_all.20.in_ref), custom_call_target="tpu_custom_call" | custom-call | tf_op jit(solution)/shard_map/share/pallas_call | solution.py:179
  92.6 25.1 %all_to_all.21.in_ref = bf16[32,8,256]{2,1,0:T(8,128)(2,1)} all-to-all(bf16[32,8,256]{2,1,0:T(8,128)(2,1)} %share.1), channel_id=1, replica_groups=mesh['z'=16,'y'=4,'x'=4,'c'=2] {'z','c'}, dimensions={0} | all-to-all | bytes 262144 | tf_op jit(solution)/shard_map/all_to_all | solution.py:186
  117.7 1.8 %combine.1 = bf16[24,192]{1,0:T(8,128)(2,1)} custom-call(s32[1]{0:T(128)} %bitcast.core_ref, bf16[256,24]{1,0:T(8,128)(2,1)} %get-tuple-element.9.place_ref, bf16[32,8,256]{2,1,0:T(8,128)(2,1)} %all_to_all.21.in_ref), custom_call_target="tpu_custom_call" | custom-call | tf_op jit(solution)/shard_map/combine/pallas_call | solution.py:187
Async XLA Ops:
  0.0 60.8 %copy-start = (bf16[6144,128]{1,0:T(8,128)(2,1)S(1)}, bf16[6144,128]{1,0:T(8,128)(2,1)}, u32[]{:S(2)}) copy-start(bf16[6144,128]{1,0:T(8,128)(2,1)} %gate_a.1) | copy-start | bytes 4718596
  0.0 60.8 %copy-start.3 = (bf16[6144,8]{0,1:T(8,128)(2,1)S(1)}, bf16[6144,8]{0,1:T(8,128)(2,1)}, u32[]{:S(2)}) copy-start(bf16[6144,8]{0,1:T(8,128)(2,1)} %param.8) | copy-start | bytes 294916
  2.0 32.6 %all-to-all-start = ((bf16[32,8,256]{2,1,0:T(8,128)(2,1)}), bf16[32,8,256]{2,1,0:T(8,128)(2,1)S(1)}, u32[]{:S(2)}, u32[]{:S(2)}) async-start(bf16[32,8,256]{2,1,0:T(8,128)(2,1)} %get-tuple-element.10), calls=%async_computation | async-start | bytes 262144 | tf_op jit(solution)/shard_map/all_to_all | solution.py:158
  18.8 25.6 %collective-permute-start = (bf16[6144,128]{1,0:T(8,128)(2,1)}, bf16[6144,128]{1,0:T(8,128)(2,1)}, u32[]{:S(2)}, u32[]{:S(2)}) collective-permute-start(bf16[6144,128]{1,0:T(8,128)(2,1)} %gate_a.1), channel_id=1, source_target_pairs={{0,1},{1,0},{2,3},{3,2},{4,5},{5,4},{6,7},{7,6},{8,9},{9,8},{10,11... | collective-permute-start | bytes 4718600 | tf_op jit(solution)/shard_map/ppermute | solution.py:145
  20.9 23.5 %collective-permute-start.1 = (bf16[6144,128]{1,0:T(8,128)(2,1)}, bf16[6144,128]{1,0:T(8,128)(2,1)}, u32[]{:S(2)}, u32[]{:S(2)}) collective-permute-start(bf16[6144,128]{1,0:T(8,128)(2,1)} %up_a.1), channel_id=1, source_target_pairs={{0,1},{1,0},{2,3},{3,2},{4,5},{5,4},{6,7},{7,6},{8,9},{9,8},{10,11... | collective-permute-start | bytes 4718600 | tf_op jit(solution)/shard_map/ppermute | solution.py:146
  23.1 21.3 %collective-permute-start.2 = (bf16[128,6144]{1,0:T(8,128)(2,1)}, bf16[128,6144]{1,0:T(8,128)(2,1)}, u32[]{:S(2)}, u32[]{:S(2)}) collective-permute-start(bf16[128,6144]{1,0:T(8,128)(2,1)} %down_a.1), channel_id=1, source_target_pairs={{0,1},{1,0},{2,3},{3,2},{4,5},{5,4},{6,7},{7,6},{8,9},{9,8},{10,11... | collective-permute-start | bytes 4718600 | tf_op jit(solution)/shard_map/ppermute | solution.py:147
  34.6 0.7 copy-start.5
  37.5 23.4 %copy-start.4 = (f32[96,128]{1,0:T(8,128)S(1)}, f32[96,128]{1,0:T(8,128)}, u32[]{:S(2)}) copy-start(f32[96,128]{1,0:T(8,128)} %get-tuple-element.12.info_ref) | copy-start | bytes 147460
  37.5 23.3 %all-to-all-start.1 = ((bf16[16,96,384]{2,1,0:T(8,128)(2,1)}), bf16[16,96,384]{2,1,0:T(8,128)(2,1)S(1)}, u32[]{:S(2)}, u32[]{:S(2)}) async-start(bf16[16,96,384]{2,1,0:T(8,128)(2,1)} %get-tuple-element.11), calls=%async_computation.1 | async-start | bytes 2359296 | tf_op jit(solution)/shard_map/all_to_all | solution.py:169
  60.8 1.4 %copy-start.1 = (bf16[6144,128]{1,0:T(8,128)(2,1)S(1)}, bf16[6144,128]{1,0:T(8,128)(2,1)}, u32[]{:S(2)}) copy-start(bf16[6144,128]{1,0:T(8,128)(2,1)} %up_a.1) | copy-start | bytes 4718596
  62.3 1.4 %copy-start.2 = (bf16[128,6144]{1,0:T(8,128)(2,1)S(1)}, bf16[128,6144]{1,0:T(8,128)(2,1)}, u32[]{:S(2)}) copy-start(bf16[128,6144]{1,0:T(8,128)(2,1)} %down_a.1) | copy-start | bytes 4718596

commit v2 on v1

v2 whole, which is shorter than its diff:
```python
import jax
import jax.numpy as jnp
from jax import lax
from jax.experimental import pallas as pl
from jax.experimental.pallas import tpu as pltpu
from jax.sharding import Mesh, PartitionSpec as P

EXPERTS = 8
HALF = 6
PLANES = 16
CHIPS = 16
ROWS = PLANES * HALF
TOK = 24
FEAT = 192
PAIR = 384
D = 6144
PAY = 24
PAYS = PLANES * PAY
UNITS = 256
PACK = ROWS + ROWS // 2
PER = 4
GROUPS = CHIPS // PER
GROUP = PER * PAIR
F32 = jnp.float32
BF16 = jnp.bfloat16


def vmem():
    return pl.BlockSpec(memory_space=pltpu.VMEM)


def smem():
    return pl.BlockSpec(memory_space=pltpu.SMEM)


def hbm():
    return pl.BlockSpec(memory_space=pltpu.HBM)


def anyspace():
    return pl.BlockSpec(memory_space=pl.ANY)


def small():
    return pltpu.CompilerParams(vmem_limit_bytes=8 << 20)


def iota(shape, dim):
    return lax.broadcasted_iota(jnp.int32, shape, dim)


def onehot(mask):
    return mask.astype(F32).astype(BF16)


def dot_nt(a, b):
    return lax.dot_general(a, b, (((1,), (1,)), ((), ())), preferred_element_type=F32)


def dot_tn(a, b):
    return lax.dot_general(a, b, (((0,), (0,)), ((), ())), preferred_element_type=F32)


def dot_nn(a, b):
    return jnp.dot(a, b, preferred_element_type=F32)


def ranks(routes_ref):
    first = routes_ref[0:1, :]
    second = routes_ref[1:2, :]
    k8 = iota((EXPERTS, TOK), 0)
    named = onehot((k8 == first) | (k8 == second))
    earlier = onehot(iota((TOK, TOK), 0) < iota((TOK, TOK), 1))
    rank = dot_nn(named, earlier)
    rank = jnp.where(named.astype(F32) > 0.5, rank, 100.0).astype(BF16)
    plane = iota((PLANES, PAY, EXPERTS), 0).reshape(PAYS, EXPERTS)
    pick = onehot((plane >> 1) == iota((PAYS, EXPERTS), 1))
    rank_row = dot_nn(pick, rank)
    i = iota((PLANES, PAY, TOK), 1).reshape(PAYS, TOK)
    return rank_row, i


def dispatch_kernel(core_ref, routes_ref, tok_ref, out_ref):
    core = core_ref[0]
    rank_row, i = ranks(routes_ref)
    first = routes_ref[0:1, :]
    second = routes_ref[1:2, :]
    is_a = i < 12
    is_b = (i >= 12) & (i < 18)
    slot = jnp.where(is_a, i, jnp.where(is_b, i - 12, i - 18))
    hit_low = rank_row == slot.astype(F32)
    hit_high = (rank_row == (slot + HALF).astype(F32)) & (i >= 12)
    tok = tok_ref[...].astype(F32)
    zero = jnp.zeros((TOK, 64), F32)
    part_a = jnp.where(core == 0, tok[:, :128], tok[:, 64:]).astype(BF16)
    head = jnp.concatenate([tok[:, :64], zero], axis=1)
    tail = jnp.concatenate([tok[:, 128:], zero], axis=1)
    part_b = jnp.where(core == 0, tail, head)
    part_b_high = pltpu.roll(part_b, 64, 1).astype(BF16)
    part_b = part_b.astype(BF16)
    lane = iota((128, TOK), 0)
    marks = onehot((lane == first) | (lane == second))
    marks_high = onehot((lane - 64 == first) | (lane - 64 == second))
    payload = dot_nn(onehot(hit_low & is_a), part_a)
    payload = payload + dot_nn(onehot(hit_low & is_b), part_b)
    payload = payload + dot_nn(onehot(hit_high & is_b), part_b_high)
    payload = payload + dot_nt(onehot(hit_low & (i >= 18)), marks)
    payload = payload + dot_nt(onehot(hit_high & (i >= 18)), marks_high)
    out_ref[...] = payload.reshape(PLANES, PAY, 128).astype(BF16)


def place_kernel(routes_ref, out_ref):
    rank_row, i = ranks(routes_ref)
    low = rank_row == (i - 12).astype(F32)
    high = rank_row == (i - 12 + HALF).astype(F32)
    inside = (i >= 12) & (i < 18)
    out_ref[0] = onehot((rank_row == i.astype(F32)) & (i < 12))
    out_ref[1] = onehot(low & inside)
    out_ref[2] = onehot(high & inside)


def repack_kernel(core_ref, in_ref, out_ref, info_ref, block_ref, sem):
    core = core_ref[0]
    x = in_ref[...].astype(F32).reshape(PAYS, 128).astype(BF16)
    p = iota((ROWS, PAYS), 0)
    at = iota((ROWS, PAYS), 1) - p - (PAY - HALF) * ((p * 43) >> 8)
    rest = dot_nn(onehot(at == 12), x)
    near = rest[: ROWS // 2]
    far = rest[ROWS // 2 :]
    left = (iota((ROWS // 2, 128), 1) < 64) == (core == 0)
    near_roll = pltpu.roll(near, 64, 1)
    far_roll = pltpu.roll(far, 64, 1)
    even_near = jnp.where(core == 0, near, near_roll)
    even_far = jnp.where(core == 0, far_roll, far)
    odd_near = jnp.where(core == 0, near_roll, near)
    odd_far = jnp.where(core == 0, far, far_roll)
    block_ref[0, :ROWS] = dot_nn(onehot(at == 0), x).astype(BF16)
    block_ref[0, ROWS:] = jnp.where(left, even_near, even_far).astype(BF16)
    copies = [
        pltpu.make_async_copy(block_ref.at[n % 2], out_ref.at[n], sem.at[n])
        for n in range(2 * CHIPS)
    ]
    for copy in copies[0::2]:
        copy.start()
    block_ref[1, :ROWS] = dot_nn(onehot(at == HALF), x).astype(BF16)
    block_ref[1, ROWS:] = jnp.where(left, odd_near, odd_far).astype(BF16)
    for copy in copies[1::2]:
        copy.start()
    info = dot_nn(onehot(at == 18), x)
    info_ref[...] = jnp.where(core == 0, info, pltpu.roll(info, 64, 1))
    for copy in copies:
        copy.wait()


def expert_kernel(
    expert_ref, x_ref, info_ref, router_ref, gate_a, gate_b, up_a, up_b, down_a, down_b,
    out_ref, wide_ref, down_ref, wide_sem, down_sem,
):
    expert = expert_ref[0]
    wide_copies = []
    down_copies = []
    for g in range(GROUPS):
        rows = pl.ds(g * GROUP, GROUP)
        for n, src in enumerate((gate_a, gate_b, up_a, up_b)):
            wide_copies.append(
                pltpu.make_async_copy(src.at[rows, :], wide_ref.at[n, rows, :], wide_sem.at[g, n])
            )
    for g in range(GROUPS):
        cols = pl.ds(g * GROUP, GROUP)
        for n, src in enumerate((down_a, down_b)):
            down_copies.append(
                pltpu.make_async_copy(
                    src.at[:, cols], down_ref.at[pl.ds(128 * n, 128), cols], down_sem.at[g, n]
                )
            )
    for copy in wide_copies + down_copies:
        copy.start()
    left = iota((ROWS // 2, 128), 1) < 64
    xs = []
    logits = jnp.zeros((ROWS, EXPERTS), F32)
    for g in range(GROUPS):
        parts = []
        for chip in range(g * PER, (g + 1) * PER):
            rest_a = x_ref[2 * chip, ROWS:].astype(F32)
            rest_b = x_ref[2 * chip + 1, ROWS:].astype(F32)
            near = jnp.where(left, rest_a, rest_b)
            far = pltpu.roll(jnp.where(left, rest_b, rest_a), 64, 1)
            middle = jnp.concatenate([near, far], axis=0).astype(BF16)
            parts += [x_ref[2 * chip, :ROWS], middle, x_ref[2 * chip + 1, :ROWS]]
        x = jnp.concatenate(parts, axis=1)
        xs.append(x)
        logits = logits + dot_nt(x, router_ref[:, g * GROUP : (g + 1) * GROUP])
    k = iota((ROWS, EXPERTS), 1)
    named = info_ref[:, :EXPERTS]
    other = jnp.sum(jnp.where((k != expert) & (named > 0.5), logits, 0.0), axis=1, keepdims=True)
    own = jnp.sum(jnp.where(k == expert, logits, 0.0), axis=1, keepdims=True)
    weight = 1.0 / (1.0 + jnp.exp(other - own))
    gate = jnp.zeros((ROWS, UNITS), F32)
    up = jnp.zeros((ROWS, UNITS), F32)
    for g in range(GROUPS):
        for n in range(4):
            wide_copies[g * 4 + n].wait()
        rows = slice(g * GROUP, (g + 1) * GROUP)
        x = xs[g]
        gate = gate + dot_nn(x, jnp.concatenate([wide_ref[0, rows, :], wide_ref[1, rows, :]], axis=1))
        up = up + dot_nn(x, jnp.concatenate([wide_ref[2, rows, :], wide_ref[3, rows, :]], axis=1))
    hidden = (gate / (1.0 + jnp.exp(-gate)) * up * weight).astype(BF16)
    for g in range(GROUPS):
        for n in range(2):
            down_copies[g * 2 + n].wait()
        terms = dot_nn(hidden, down_ref[:, g * GROUP : (g + 1) * GROUP])
        for n in range(PER):
            chip = g * PER + n
            base = n * PAIR
            near = terms[: ROWS // 2, base + 128 : base + 256]
            far = pltpu.roll(terms[ROWS // 2 :, base + 128 : base + 256], 64, 1)
            out_ref[2 * chip, :ROWS] = terms[:, base : base + 128].astype(BF16)
            out_ref[2 * chip, ROWS:] = jnp.where(left, near, far).astype(BF16)
            out_ref[2 * chip + 1, :ROWS] = terms[:, base + 256 : base + 384].astype(BF16)
            out_ref[2 * chip + 1, ROWS:] = jnp.where(left, far, near).astype(BF16)


def share_kernel(core_ref, in_ref, out_ref):
    core = core_ref[0]
    halves = []
    for half in range(2):
        total = in_ref[half].astype(F32)
        for chip in range(1, CHIPS):
            total = total + in_ref[2 * chip + half].astype(F32)
        halves.append(total)
    even = halves[0][ROWS:]
    odd = halves[1][ROWS:]
    left = iota((ROWS // 2, 128), 1) < 64
    low = jnp.where(left, even, pltpu.roll(odd, 64, 1))
    high = jnp.where(left, pltpu.roll(even, 64, 1), odd)
    near = jnp.where(core == 0, low, high)
    far = jnp.where(core == 0, high, low)
    rest = jnp.concatenate([near, far], axis=0).astype(BF16)
    p = iota((PAYS, ROWS), 1)
    at = iota((PAYS, ROWS), 0) - p - (PAY - HALF) * ((p * 43) >> 8)
    spread = dot_nn(onehot(at == 0), halves[0][:ROWS].astype(BF16))
    spread = spread + dot_nn(onehot(at == HALF), halves[1][:ROWS].astype(BF16))
    spread = spread + dot_nn(onehot(at == 2 * HALF), rest)
    out_ref[...] = spread.reshape(PLANES, PAY, 128).astype(BF16)


def combine_kernel(core_ref, place_ref, in_ref, out_ref):
    core = core_ref[0]
    x = in_ref[...].astype(F32).reshape(PAYS, 128).astype(BF16)
    side = dot_tn(place_ref[0], x)
    low = dot_tn(place_ref[1], x)
    high = pltpu.roll(dot_tn(place_ref[2], x), 64, 1)
    rest = (low + high)[:, :64]
    even = jnp.concatenate([side, rest], axis=1)
    odd = jnp.concatenate([rest, side], axis=1)
    out_ref[...] = jnp.where(core == 0, even, odd).astype(BF16)


def local(tokens, routes, w_router, w_gate, w_up, w_down):
    core = lax.axis_index("c").reshape(1).astype(jnp.int32)
    expert = (lax.axis_index("z") >> 1).reshape(1).astype(jnp.int32)
    swap = [(0, 1), (1, 0)]
    routes_t = routes.T
    payload = pl.pallas_call(
        dispatch_kernel,
        out_shape=jax.ShapeDtypeStruct((PLANES, PAY, 128), BF16),
        in_specs=[smem(), vmem(), vmem()],
        out_specs=vmem(),
        name="dispatch",
    )(core, routes_t, tokens)
    gate_b = lax.ppermute(w_gate, "c", swap)
    up_b = lax.ppermute(w_up, "c", swap)
    down_b = lax.ppermute(w_down, "c", swap)
    place = pl.pallas_call(
        place_kernel,
        out_shape=jax.ShapeDtypeStruct((3, PAYS, TOK), BF16),
        in_specs=[vmem()],
        out_specs=vmem(),
        name="place",
    )(routes_t)
    arrived = lax.all_to_all(payload, "z", 0, 0, tiled=True)
    blocks, info = pl.pallas_call(
        repack_kernel,
        out_shape=(
            jax.ShapeDtypeStruct((2 * CHIPS, PACK, 128), BF16),
            jax.ShapeDtypeStruct((ROWS, 128), F32),
        ),
        in_specs=[smem(), vmem()],
        out_specs=(anyspace(), vmem()),
        scratch_shapes=[pltpu.VMEM((2, PACK, 128), BF16), pltpu.SemaphoreType.DMA((2 * CHIPS,))],
        cost_estimate=pl.CostEstimate(flops=100000000000, transcendentals=0, bytes_accessed=1048576),
        name="repack",
    )(core, arrived)
    gathered = lax.all_to_all(blocks, ("y", "x", "c"), 0, 0, tiled=True)
    terms = pl.pallas_call(
        expert_kernel,
        out_shape=jax.ShapeDtypeStruct((2 * CHIPS, PACK, 128), BF16),
        in_specs=[smem()] + [vmem()] * 3 + [hbm()] * 6,
        out_specs=vmem(),
        scratch_shapes=[
            pltpu.VMEM((4, D, 128), BF16),
            pltpu.VMEM((UNITS, D), BF16),
            pltpu.SemaphoreType.DMA((GROUPS, 4)),
            pltpu.SemaphoreType.DMA((GROUPS, 2)),
        ],
        compiler_params=pltpu.CompilerParams(vmem_limit_bytes=48 << 20),
        name="expert",
    )(expert, gathered, info, w_router.T, w_gate, gate_b, w_up, up_b, w_down, down_b)
    parts = lax.all_to_all(terms, ("y", "x", "c"), 0, 0, tiled=True)
    shares = pl.pallas_call(
        share_kernel,
        out_shape=jax.ShapeDtypeStruct((PLANES, PAY, 128), BF16),
        in_specs=[smem(), vmem()],
        out_specs=vmem(),
        compiler_params=small(),
        name="share",
    )(core, parts)
    back = lax.all_to_all(shares, "z", 0, 0, tiled=True)
    return pl.pallas_call(
        combine_kernel,
        out_shape=jax.ShapeDtypeStruct((TOK, FEAT), BF16),
        in_specs=[smem(), vmem(), vmem()],
        out_specs=vmem(),
        compiler_params=small(),
        name="combine",
    )(core, place, back)


def solution(mesh):
    fine = Mesh(mesh.devices.reshape(16, 4, 4, 2), ("z", "y", "x", "c"))
    shard = ("y", "x", "c")
    both = ("z",) + shard
    return jax.shard_map(
        local,
        mesh=fine,
        in_specs=(P("z", shard), P("z", None), P(), P(None, both), P(None, both), P(both, None)),
        out_specs=P("z", shard),
        check_vma=False,
    )
```

time: 120 us -> 111 us (0.925)
  blocking collectives: 47 us -> 23.3 us
  starting transfers between devices: 30.1 us -> 37.4 us
  waiting for transfers between devices: 25.8 us -> 32.5 us
  local copies, waits for them, and re-layouts: 3.48 us -> 1.63 us
  Pallas kernels: 13 us -> 14.8 us
    all_to_all x2 -> x1, blocking collectives: 47 us -> 23.3 us  [local(): parts = lax.all_to_all(terms, ('y', 'x', 'c'), 0, 0, tiled=True)]
    all_to_all x2 -> x3, waiting for transfers between devices: 25.8 us -> 32.5 us  [the longest x1 17.7 us: local(): gathered = lax.all_to_all(blocks, ('y', 'x', 'c'), 0, 0, tiled=True)]
    all_to_all x2 -> x3, starting transfers between devices: 23.6 us -> 30.2 us  [the longest x1 15.7 us: local(): arrived = lax.all_to_all(payload, 'z', 0, 0, tiled=True)]
    pallas_call x4 -> x5, Pallas kernels: 11.2 us -> 13.9 us  [the longest x1 6.2 us: local(): pl.pallas_call(expert_kernel, out_shape=jax.ShapeDtypeStruct((2 * CHIPS,...]
    unnamed x12 -> x10, local copies, waits for them, and re-layouts: 3.48 us -> 1.63 us
  transfers between devices with their start and end apart: 5 -> 6, of which waited for: 2 -> 3; matrix products, arithmetic and copies ran while one was open for 0% -> 0% of each run, Pallas kernels for 2% -> 4%
where the time goes in v2:
time: 111 us; the launch traced here: 110 us
  starting transfers between devices  37.4 us (34%)
  waiting for transfers between devices  32.5 us (29%)
  blocking collectives  23.3 us (21%)
  Pallas kernels  14.8 us (13%)
  local copies, waits for them, and re-layouts  1.63 us (1%)
    all_to_all x1, blocking collectives, local(): parts = lax.all_to_all(terms, ('y', 'x', 'c'), 0, 0, tiled=True)  23.3 us
    all_to_all x1, waiting for transfers between devices, local(): gathered = lax.all_to_all(blocks, ('y', 'x', 'c'), 0, 0, tiled=True)  17.7 us
    all_to_all x1, starting transfers between devices, local(): arrived = lax.all_to_all(payload, 'z', 0, 0, tiled=True)  15.7 us
    all_to_all x1, waiting for transfers between devices, local(): back = lax.all_to_all(shares, 'z', 0, 0, tiled=True)  10.2 us
    all_to_all x1, starting transfers between devices, local(): gathered = lax.all_to_all(blocks, ('y', 'x', 'c'), 0, 0, tiled=True)  9.89 us
    pallas_call x1, Pallas kernels, local(): pl.pallas_call(expert_kernel, out_shape=jax.ShapeDtypeStruct((2 * CHIPS,...  6.2 us
    all_to_all x1, waiting for transfers between devices, local(): arrived = lax.all_to_all(payload, 'z', 0, 0, tiled=True)  4.63 us
    all_to_all x1, starting transfers between devices, local(): back = lax.all_to_all(shares, 'z', 0, 0, tiled=True)  4.57 us
  transfers between devices with their start and end apart: 6, of which 3 were waited for; matrix products, arithmetic and copies ran while one was open for 0% of the time, Pallas kernels for 4%

profile of v2, /device:TPU:1, one launch (start us, length us, event | category | flops | bytes accessed | tf_op | source)
XLA Modules:
  0.0 109.7 jit_solution(3459053105147910831)
XLA Ops:
  0.0 1.9 %dispatch.1 = bf16[16,24,128]{2,1,0:T(8,128)(2,1)} custom-call(s32[1]{0:T(128)} %bitcast.core_ref, s32[2,24]{1,0:T(2,128)} %bitcast.5, bf16[24,192]{1,0:T(8,128)(2,1)} %tok_ref.1), custom_call_target="tpu_custom_call" | custom-call | tf_op jit(solution)/shard_map/dispatch/pallas_call | solution.py:264
  1.9 15.7 %all-to-all-start = ((bf16[16,24,128]{2,1,0:T(8,128)(2,1)}), bf16[16,24,128]{2,1,0:T(8,128)(2,1)S(1)}, u32[]{:S(2)}, u32[]{:S(2)}) async-start(bf16[16,24,128]{2,1,0:T(8,128)(2,1)} %dispatch.1), calls=%async_computation | async-start | bytes 196608 | tf_op jit(solution)/shard_map/all_to_all | solution.py:281
  17.7 2.9 %collective-permute-start = (bf16[6144,128]{1,0:T(8,128)(2,1)}, bf16[6144,128]{1,0:T(8,128)(2,1)}, u32[]{:S(2)}, u32[]{:S(2)}) collective-permute-start(bf16[6144,128]{1,0:T(8,128)(2,1)} %gate_a.1), channel_id=1, source_target_pairs={{0,1},{1,0},{2,3},{3,2},{4,5},{5,4},{6,7},{7,6},{8,9},{9,8},{10,11... | collective-permute-start | bytes 4718600 | tf_op jit(solution)/shard_map/ppermute | solution.py:271
  20.5 1.9 %collective-permute-start.1 = (bf16[6144,128]{1,0:T(8,128)(2,1)}, bf16[6144,128]{1,0:T(8,128)(2,1)}, u32[]{:S(2)}, u32[]{:S(2)}) collective-permute-start(bf16[6144,128]{1,0:T(8,128)(2,1)} %up_a.1), channel_id=1, source_target_pairs={{0,1},{1,0},{2,3},{3,2},{4,5},{5,4},{6,7},{7,6},{8,9},{9,8},{10,11... | collective-permute-start | bytes 4718600 | tf_op jit(solution)/shard_map/ppermute | solution.py:272
  22.5 2.4 %collective-permute-start.2 = (bf16[128,6144]{1,0:T(8,128)(2,1)}, bf16[128,6144]{1,0:T(8,128)(2,1)}, u32[]{:S(2)}, u32[]{:S(2)}) collective-permute-start(bf16[128,6144]{1,0:T(8,128)(2,1)} %down_a.1), channel_id=1, source_target_pairs={{0,1},{1,0},{2,3},{3,2},{4,5},{5,4},{6,7},{7,6},{8,9},{9,8},{10,11... | collective-permute-start | bytes 4718600 | tf_op jit(solution)/shard_map/ppermute | solution.py:273
  24.9 4.6 %all-to-all-done.in_ref = bf16[16,24,128]{2,1,0:T(8,128)(2,1)S(1)} async-done(((bf16[16,24,128]{2,1,0:T(8,128)(2,1)}), bf16[16,24,128]{2,1,0:T(8,128)(2,1)S(1)}, u32[]{:S(2)}, u32[]{:S(2)}) %all-to-all-start) | async-done | bytes 98336 | tf_op jit(solution)/shard_map/all_to_all | solution.py:281
  29.5 0.0 copy-start.4
  29.5 0.6 copy-done.4
  30.2 3.1 %repack.1 = (bf16[32,144,128]{2,1,0:T(8,128)(2,1)}, f32[96,128]{1,0:T(8,128)}) custom-call(s32[1]{0:T(128)} %bitcast.core_ref, bf16[16,24,128]{2,1,0:T(8,128)(2,1)} %copy-done.4), custom_call_target="tpu_custom_call" | custom-call | flops 99999997952 | bytes 1048576 | tf_op jit(solution)/shard_map/repack/pallas_call | solution.py:282
  33.3 0.0 copy-start
  33.3 0.0 copy-start.2
  33.3 0.0 copy-start.3
  33.3 9.9 %all-to-all-start.1 = ((bf16[32,144,128]{2,1,0:T(8,128)(2,1)}), bf16[32,144,128]{2,1,0:T(8,128)(2,1)S(1)}, u32[]{:S(2)}, u32[]{:S(2)}) async-start(bf16[32,144,128]{2,1,0:T(8,128)(2,1)} %get-tuple-element.7), calls=%async_computation.1 | async-start | bytes 2359296 | tf_op jit(solution)/shard_map/all_to_all | solution.py:294
  43.2 17.7 %all-to-all-done.1.x_ref = bf16[32,144,128]{2,1,0:T(8,128)(2,1)S(1)} async-done(((bf16[32,144,128]{2,1,0:T(8,128)(2,1)}), bf16[32,144,128]{2,1,0:T(8,128)(2,1)S(1)}, u32[]{:S(2)}, u32[]{:S(2)}) %all-to-all-start.1) | async-done | bytes 1179680 | tf_op jit(solution)/shard_map/all_to_all | solution.py:294
  60.9 0.0 collective-permute-done.gate_b
  60.9 0.0 collective-permute-done.1.up_b
  60.9 0.0 collective-permute-done.2.down_b
  60.9 0.0 copy-done
  60.9 0.0 copy-done.2
  60.9 0.0 copy-done.3
  60.9 6.2 %expert.1 = bf16[32,144,128]{2,1,0:T(8,128)(2,1)S(1)} custom-call(s32[1]{0:T(128)} %bitcast.2.expert_ref, bf16[32,144,128]{2,1,0:T(8,128)(2,1)S(1)} %all-to-all-done.1.x_ref, f32[96,128]{1,0:T(8,128)S(1)} %copy-done.3, bf16[8,6144]{1,0:T(8,128)(2,1)S(1)} %bitcast.4, bf16[6144,128]{1,0:T(8,128)(2,1)S(1)} %copy-done, ...), custom_call_target="tpu_custom_call" | custom-call | tf_op jit(solution)/shard_map/expert/pallas_call | solution.py:295
  67.1 23.3 %all_to_all.20.in_ref = bf16[32,144,128]{2,1,0:T(8,128)(2,1)S(1)} all-to-all(bf16[32,144,128]{2,1,0:T(8,128)(2,1)S(1)} %expert.1), channel_id=1, replica_groups=mesh['z'=16,'y'=4,'x'=4,'c'=2] {'y','x','c'}, dimensions={0} | all-to-all | bytes 2359296 | tf_op jit(solution)/shard_map/all_to_all | solution.py:309
  90.4 1.0 share.1
  91.4 4.6 %all-to-all-start.3 = ((bf16[16,24,128]{2,1,0:T(8,128)(2,1)}), bf16[16,24,128]{2,1,0:T(8,128)(2,1)S(1)}, u32[]{:S(2)}, u32[]{:S(2)}) async-start(bf16[16,24,128]{2,1,0:T(8,128)(2,1)} %share.1), calls=%async_computation.3 | async-start | bytes 196608 | tf_op jit(solution)/shard_map/all_to_all | solution.py:318
  96.0 1.7 %place.1.place_ref = bf16[3,384,24]{2,1,0:T(8,128)(2,1)} custom-call(s32[2,24]{1,0:T(2,128)} %bitcast.6), custom_call_target="tpu_custom_call" | custom-call | tf_op jit(solution)/shard_map/place/pallas_call | solution.py:274
  97.7 10.2 %all-to-all-done.3.in_ref = bf16[16,24,128]{2,1,0:T(8,128)(2,1)S(1)} async-done(((bf16[16,24,128]{2,1,0:T(8,128)(2,1)}), bf16[16,24,128]{2,1,0:T(8,128)(2,1)S(1)}, u32[]{:S(2)}, u32[]{:S(2)}) %all-to-all-start.3) | async-done | bytes 98336 | tf_op jit(solution)/shard_map/all_to_all | solution.py:318
  107.9 0.0 copy-start.1
  107.9 1.0 copy-done.1
  108.9 0.9 combine.1
Async XLA Ops:
  1.9 27.6 %all-to-all-start = ((bf16[16,24,128]{2,1,0:T(8,128)(2,1)}), bf16[16,24,128]{2,1,0:T(8,128)(2,1)S(1)}, u32[]{:S(2)}, u32[]{:S(2)}) async-start(bf16[16,24,128]{2,1,0:T(8,128)(2,1)} %dispatch.1), calls=%async_computation | async-start | bytes 196608 | tf_op jit(solution)/shard_map/all_to_all | solution.py:281
  17.7 43.2 %collective-permute-start = (bf16[6144,128]{1,0:T(8,128)(2,1)}, bf16[6144,128]{1,0:T(8,128)(2,1)}, u32[]{:S(2)}, u32[]{:S(2)}) collective-permute-start(bf16[6144,128]{1,0:T(8,128)(2,1)} %gate_a.1), channel_id=1, source_target_pairs={{0,1},{1,0},{2,3},{3,2},{4,5},{5,4},{6,7},{7,6},{8,9},{9,8},{10,11... | collective-permute-start | bytes 4718600 | tf_op jit(solution)/shard_map/ppermute | solution.py:271
  20.5 40.4 %collective-permute-start.1 = (bf16[6144,128]{1,0:T(8,128)(2,1)}, bf16[6144,128]{1,0:T(8,128)(2,1)}, u32[]{:S(2)}, u32[]{:S(2)}) collective-permute-start(bf16[6144,128]{1,0:T(8,128)(2,1)} %up_a.1), channel_id=1, source_target_pairs={{0,1},{1,0},{2,3},{3,2},{4,5},{5,4},{6,7},{7,6},{8,9},{9,8},{10,11... | collective-permute-start | bytes 4718600 | tf_op jit(solution)/shard_map/ppermute | solution.py:272
  22.5 38.4 %collective-permute-start.2 = (bf16[128,6144]{1,0:T(8,128)(2,1)}, bf16[128,6144]{1,0:T(8,128)(2,1)}, u32[]{:S(2)}, u32[]{:S(2)}) collective-permute-start(bf16[128,6144]{1,0:T(8,128)(2,1)} %down_a.1), channel_id=1, source_target_pairs={{0,1},{1,0},{2,3},{3,2},{4,5},{5,4},{6,7},{7,6},{8,9},{9,8},{10,11... | collective-permute-start | bytes 4718600 | tf_op jit(solution)/shard_map/ppermute | solution.py:273
  29.5 0.7 copy-start.4
  33.3 27.6 %copy-start = (bf16[6144,128]{1,0:T(8,128)(2,1)S(1)}, bf16[6144,128]{1,0:T(8,128)(2,1)}, u32[]{:S(2)}) copy-start(bf16[6144,128]{1,0:T(8,128)(2,1)} %gate_a.1) | copy-start | bytes 4718596
  33.3 27.6 %copy-start.2 = (bf16[6144,8]{0,1:T(8,128)(2,1)S(1)}, bf16[6144,8]{0,1:T(8,128)(2,1)}, u32[]{:S(2)}) copy-start(bf16[6144,8]{0,1:T(8,128)(2,1)} %param.8) | copy-start | bytes 294916
  33.3 27.6 %copy-start.3 = (f32[96,128]{1,0:T(8,128)S(1)}, f32[96,128]{1,0:T(8,128)}, u32[]{:S(2)}) copy-start(f32[96,128]{1,0:T(8,128)} %get-tuple-element.8.info_ref) | copy-start | bytes 147460
  33.3 27.6 %all-to-all-start.1 = ((bf16[32,144,128]{2,1,0:T(8,128)(2,1)}), bf16[32,144,128]{2,1,0:T(8,128)(2,1)S(1)}, u32[]{:S(2)}, u32[]{:S(2)}) async-start(bf16[32,144,128]{2,1,0:T(8,128)(2,1)} %get-tuple-element.7), calls=%async_computation.1 | async-start | bytes 2359296 | tf_op jit(solution)/shard_map/all_to_all | solution.py:294
  91.4 16.5 %all-to-all-start.3 = ((bf16[16,24,128]{2,1,0:T(8,128)(2,1)}), bf16[16,24,128]{2,1,0:T(8,128)(2,1)S(1)}, u32[]{:S(2)}, u32[]{:S(2)}) async-start(bf16[16,24,128]{2,1,0:T(8,128)(2,1)} %share.1), calls=%async_computation.3 | async-start | bytes 196608 | tf_op jit(solution)/shard_map/all_to_all | solution.py:318
  107.9 1.0 copy-start.1

commit v3 on v2

--- a/solution.py
+++ b/solution.py
@@ -18,7 +18,7 @@
 PAYS = PLANES * PAY
 UNITS = 256
 PACK = ROWS + ROWS // 2
-PER = 4
+PER = 16
 GROUPS = CHIPS // PER
 GROUP = PER * PAIR
 F32 = jnp.float32
@@ -80,8 +80,8 @@
     return rank_row, i
 
 
-def dispatch_kernel(core_ref, routes_ref, tok_ref, out_ref):
-    core = core_ref[0]
+def dispatch_kernel(routes_ref, tok_ref, out_ref):
+    core = lax.axis_index("c")
     rank_row, i = ranks(routes_ref)
     first = routes_ref[0:1, :]
     second = routes_ref[1:2, :]
@@ -119,8 +119,8 @@
     out_ref[2] = onehot(high & inside)
 
 
-def repack_kernel(core_ref, in_ref, out_ref, info_ref, block_ref, sem):
-    core = core_ref[0]
+def repack_kernel(in_ref, out_ref, info_ref):
+    core = lax.axis_index("c")
     x = in_ref[...].astype(F32).reshape(PAYS, 128).astype(BF16)
     p = iota((ROWS, PAYS), 0)
     at = iota((ROWS, PAYS), 1) - p - (PAY - HALF) * ((p * 43) >> 8)
@@ -134,47 +134,26 @@
     even_far = jnp.where(core == 0, far_roll, far)
     odd_near = jnp.where(core == 0, near_roll, near)
     odd_far = jnp.where(core == 0, far, far_roll)
-    block_ref[0, :ROWS] = dot_nn(onehot(at == 0), x).astype(BF16)
-    block_ref[0, ROWS:] = jnp.where(left, even_near, even_far).astype(BF16)
-    copies = [
-        pltpu.make_async_copy(block_ref.at[n % 2], out_ref.at[n], sem.at[n])
-        for n in range(2 * CHIPS)
-    ]
-    for copy in copies[0::2]:
-        copy.start()
-    block_ref[1, :ROWS] = dot_nn(onehot(at == HALF), x).astype(BF16)
-    block_ref[1, ROWS:] = jnp.where(left, odd_near, odd_far).astype(BF16)
-    for copy in copies[1::2]:
-        copy.start()
+    even_rest = jnp.where(left, even_near, even_far).astype(BF16)
+    odd_rest = jnp.where(left, odd_near, odd_far).astype(BF16)
+    even = dot_nn(onehot(at == 0), x).astype(BF16)
+    odd = dot_nn(onehot(at == HALF), x).astype(BF16)
+    for chip in range(CHIPS):
+        out_ref[2 * chip, :ROWS] = even
+        out_ref[2 * chip, ROWS:] = even_rest
+        out_ref[2 * chip + 1, :ROWS] = odd
+        out_ref[2 * chip + 1, ROWS:] = odd_rest
     info = dot_nn(onehot(at == 18), x)
     info_ref[...] = jnp.where(core == 0, info, pltpu.roll(info, 64, 1))
-    for copy in copies:
-        copy.wait()
 
 
 def expert_kernel(
-    expert_ref, x_ref, info_ref, router_ref, gate_a, gate_b, up_a, up_b, down_a, down_b,
-    out_ref, wide_ref, down_ref, wide_sem, down_sem,
+    x_ref, info_ref, router_ref, gate_a, gate_b, up_a, up_b, down_a, down_b,
+    out_ref, down_v, sem,
 ):
-    expert = expert_ref[0]
-    wide_copies = []
-    down_copies = []
-    for g in range(GROUPS):
-        rows = pl.ds(g * GROUP, GROUP)
-        for n, src in enumerate((gate_a, gate_b, up_a, up_b)):
-            wide_copies.append(
-                pltpu.make_async_copy(src.at[rows, :], wide_ref.at[n, rows, :], wide_sem.at[g, n])
-            )
-    for g in range(GROUPS):
-        cols = pl.ds(g * GROUP, GROUP)
-        for n, src in enumerate((down_a, down_b)):
-            down_copies.append(
-                pltpu.make_async_copy(
-                    src.at[:, cols], down_ref.at[pl.ds(128 * n, 128), cols], down_sem.at[g, n]
-                )
-            )
-    for copy in wide_copies + down_copies:
-        copy.start()
+    expert = lax.axis_index("z") >> 1
+    copy = pltpu.make_async_copy(down_b, down_v, sem.at[0])
+    copy.start()
     left = iota((ROWS // 2, 128), 1) < 64
     xs = []
     logits = jnp.zeros((ROWS, EXPERTS), F32)
@@ -198,17 +177,16 @@
     gate = jnp.zeros((ROWS, UNITS), F32)
     up = jnp.zeros((ROWS, UNITS), F32)
     for g in range(GROUPS):
-        for n in range(4):
-            wide_copies[g * 4 + n].wait()
         rows = slice(g * GROUP, (g + 1) * GROUP)
         x = xs[g]
-        gate = gate + dot_nn(x, jnp.concatenate([wide_ref[0, rows, :], wide_ref[1, rows, :]], axis=1))
-        up = up + dot_nn(x, jnp.concatenate([wide_ref[2, rows, :], wide_ref[3, rows, :]], axis=1))
+        gate = gate + dot_nn(x, jnp.concatenate([gate_a[rows, :], gate_b[rows, :]], axis=1))
+        up = up + dot_nn(x, jnp.concatenate([up_a[rows, :], up_b[rows, :]], axis=1))
     hidden = (gate / (1.0 + jnp.exp(-gate)) * up * weight).astype(BF16)
+    copy.wait()
     for g in range(GROUPS):
-        for n in range(2):
-            down_copies[g * 2 + n].wait()
-        terms = dot_nn(hidden, down_ref[:, g * GROUP : (g + 1) * GROUP])
+        cols = slice(g * GROUP, (g + 1) * GROUP)
+        down = jnp.concatenate([down_a[:, cols], down_v[:, cols]], axis=0)
+        terms = dot_nn(hidden, down)
         for n in range(PER):
             chip = g * PER + n
             base = n * PAIR
@@ -220,8 +198,8 @@
             out_ref[2 * chip + 1, ROWS:] = jnp.where(left, far, near).astype(BF16)
 
 
-def share_kernel(core_ref, in_ref, out_ref):
-    core = core_ref[0]
+def share_kernel(in_ref, out_ref):
+    core = lax.axis_index("c")
     halves = []
     for half in range(2):
         total = in_ref[half].astype(F32)
@@ -244,8 +222,8 @@
     out_ref[...] = spread.reshape(PLANES, PAY, 128).astype(BF16)
 
 
-def combine_kernel(core_ref, place_ref, in_ref, out_ref):
-    core = core_ref[0]
+def combine_kernel(place_ref, in_ref, out_ref):
+    core = lax.axis_index("c")
     x = in_ref[...].astype(F32).reshape(PAYS, 128).astype(BF16)
     side = dot_tn(place_ref[0], x)
     low = dot_tn(place_ref[1], x)
@@ -257,17 +235,15 @@
 
 
 def local(tokens, routes, w_router, w_gate, w_up, w_down):
-    core = lax.axis_index("c").reshape(1).astype(jnp.int32)
-    expert = (lax.axis_index("z") >> 1).reshape(1).astype(jnp.int32)
     swap = [(0, 1), (1, 0)]
     routes_t = routes.T
     payload = pl.pallas_call(
         dispatch_kernel,
         out_shape=jax.ShapeDtypeStruct((PLANES, PAY, 128), BF16),
-        in_specs=[smem(), vmem(), vmem()],
+        in_specs=[vmem(), vmem()],
         out_specs=vmem(),
         name="dispatch",
-    )(core, routes_t, tokens)
+    )(routes_t, tokens)
     gate_b = lax.ppermute(w_gate, "c", swap)
     up_b = lax.ppermute(w_up, "c", swap)
     down_b = lax.ppermute(w_down, "c", swap)
@@ -285,45 +261,44 @@
             jax.ShapeDtypeStruct((2 * CHIPS, PACK, 128), BF16),
             jax.ShapeDtypeStruct((ROWS, 128), F32),
         ),
-        in_specs=[smem(), vmem()],
-        out_specs=(anyspace(), vmem()),
-        scratch_shapes=[pltpu.VMEM((2, PACK, 128), BF16), pltpu.SemaphoreType.DMA((2 * CHIPS,))],
+        in_specs=[vmem()],
+        out_specs=(vmem(), vmem()),
+        compiler_params=small(),
         cost_estimate=pl.CostEstimate(flops=100000000000, transcendentals=0, bytes_accessed=1048576),
         name="repack",
-    )(core, arrived)
+    )(arrived)
+    blocks, place = lax.optimization_barrier((blocks, place))
     gathered = lax.all_to_all(blocks, ("y", "x", "c"), 0, 0, tiled=True)
     terms = pl.pallas_call(
         expert_kernel,
         out_shape=jax.ShapeDtypeStruct((2 * CHIPS, PACK, 128), BF16),
-        in_specs=[smem()] + [vmem()] * 3 + [hbm()] * 6,
+        in_specs=[vmem()] * 8 + [hbm()],
         out_specs=vmem(),
         scratch_shapes=[
-            pltpu.VMEM((4, D, 128), BF16),
-            pltpu.VMEM((UNITS, D), BF16),
-            pltpu.SemaphoreType.DMA((GROUPS, 4)),
-            pltpu.SemaphoreType.DMA((GROUPS, 2)),
+            pltpu.VMEM((128, D), BF16),
+            pltpu.SemaphoreType.DMA((1,)),
         ],
-        compiler_params=pltpu.CompilerParams(vmem_limit_bytes=48 << 20),
+        compiler_params=pltpu.CompilerParams(vmem_limit_bytes=16 << 20),
         name="expert",
-    )(expert, gathered, info, w_router.T, w_gate, gate_b, w_up, up_b, w_down, down_b)
+    )(gathered, info, w_router.T, w_gate, gate_b, w_up, up_b, w_down, down_b)
     parts = lax.all_to_all(terms, ("y", "x", "c"), 0, 0, tiled=True)
     shares = pl.pallas_call(
         share_kernel,
         out_shape=jax.ShapeDtypeStruct((PLANES, PAY, 128), BF16),
-        in_specs=[smem(), vmem()],
+        in_specs=[vmem()],
         out_specs=vmem(),
         compiler_params=small(),
         name="share",
-    )(core, parts)
+    )(parts)
     back = lax.all_to_all(shares, "z", 0, 0, tiled=True)
     return pl.pallas_call(
         combine_kernel,
         out_shape=jax.ShapeDtypeStruct((TOK, FEAT), BF16),
-        in_specs=[smem(), vmem(), vmem()],
+        in_specs=[vmem(), vmem()],
         out_specs=vmem(),
         compiler_params=small(),
         name="combine",
-    )(core, place, back)
+    )(place, back)
 
 
 def solution(mesh):

time: 111 us -> 104 us (0.937)
  blocking collectives: 23.3 us -> 69.3 us
  waiting for transfers between devices: 32.5 us -> 2.94 us
  starting transfers between devices: 37.4 us -> 22.9 us
  Pallas kernels: 14.8 us -> 8.16 us
  local copies, waits for them, and re-layouts: 1.63 us -> 0.02 us
    all_to_all x0 -> x2, blocking collectives: none -> 46.6 us  [the longest x1 28.7 us: local(): gathered = lax.all_to_all(blocks, ('y', 'x', 'c'), 0, 0, tiled=True)]
    all_to_all x2 -> x0, waiting for transfers between devices: 27.9 us -> none  [the longest x1 17.7 us: local(): gathered = lax.all_to_all(blocks, ('y', 'x', 'c'), 0, 0, tiled=True)]
    all_to_all x2 -> x0, starting transfers between devices: 14.5 us -> none  [the longest x1 9.89 us: local(): gathered = lax.all_to_all(blocks, ('y', 'x', 'c'), 0, 0, tiled=True)]
    pallas_call x1, Pallas kernels: 6.2 us -> 3.01 us  [local(): pl.pallas_call(expert_kernel, out_shape=jax.ShapeDtypeStruct((2 * CHIPS,...]
    pallas_call x1, Pallas kernels: 3.1 us -> 0.3 us  [local(): pl.pallas_call(repack_kernel, out_shape=(jax.ShapeDtypeStruct((2 * CHIPS,...]
    all_to_all x1, waiting for transfers between devices: 4.63 us -> 2.94 us  [local(): arrived = lax.all_to_all(payload, 'z', 0, 0, tiled=True)]
    unnamed x10, local copies, waits for them, and re-layouts: 1.63 us -> 0.02 us
  transfers between devices with their start and end apart: 6 -> 4, of which waited for: 3 -> 1; matrix products, arithmetic and copies ran while one was open for 0% -> 0% of each run, Pallas kernels for 4% -> 2%
where the time goes in v3:
time: 104 us; the launch traced here: 103 us
  blocking collectives  69.3 us (67%)
  starting transfers between devices  22.9 us (22%)
  Pallas kernels  8.16 us (8%)
  waiting for transfers between devices  2.94 us (3%)
    all_to_all x1, blocking collectives, local(): gathered = lax.all_to_all(blocks, ('y', 'x', 'c'), 0, 0, tiled=True)  28.7 us
    all_to_all x1, blocking collectives, local(): parts = lax.all_to_all(terms, ('y', 'x', 'c'), 0, 0, tiled=True)  22.6 us
    all_to_all x1, blocking collectives, local(): back = lax.all_to_all(shares, 'z', 0, 0, tiled=True)  18 us
    all_to_all x1, starting transfers between devices, local(): arrived = lax.all_to_all(payload, 'z', 0, 0, tiled=True)  15.7 us
    pallas_call x1, Pallas kernels, local(): pl.pallas_call(expert_kernel, out_shape=jax.ShapeDtypeStruct((2 * CHIPS,...  3.01 us
    all_to_all x1, waiting for transfers between devices, local(): arrived = lax.all_to_all(payload, 'z', 0, 0, tiled=True)  2.94 us
    ppermute x1, starting transfers between devices, local(): gate_b = lax.ppermute(w_gate, 'c', swap)  2.87 us
    ppermute x1, starting transfers between devices, local(): down_b = lax.ppermute(w_down, 'c', swap)  2.41 us
  transfers between devices with their start and end apart: 4, of which 1 were waited for; matrix products, arithmetic and copies ran while one was open for 0% of the time, Pallas kernels for 2%

profile of v3, /device:TPU:1, one launch (start us, length us, event | category | flops | bytes accessed | tf_op | source)
XLA Modules:
  0.0 103.4 jit_solution(10425763838756799733)
XLA Ops:
  0.0 1.9 %dispatch.1 = bf16[16,24,128]{2,1,0:T(8,128)(2,1)} custom-call(s32[2,24]{1,0:T(2,128)} %bitcast.3, bf16[24,192]{1,0:T(8,128)(2,1)} %tok_ref.1), custom_call_target="tpu_custom_call" | custom-call | tf_op jit(solution)/shard_map/dispatch/pallas_call | solution.py:240
  1.9 15.7 %all-to-all-start = ((bf16[16,24,128]{2,1,0:T(8,128)(2,1)}), bf16[16,24,128]{2,1,0:T(8,128)(2,1)S(1)}, u32[]{:S(2)}, u32[]{:S(2)}) async-start(bf16[16,24,128]{2,1,0:T(8,128)(2,1)} %dispatch.1), calls=%async_computation | async-start | bytes 196608 | tf_op jit(solution)/shard_map/all_to_all | solution.py:257
  17.6 2.9 %collective-permute-start = (bf16[6144,128]{1,0:T(8,128)(2,1)}, bf16[6144,128]{1,0:T(8,128)(2,1)S(1)}, u32[]{:S(2)}, u32[]{:S(2)}) collective-permute-start(bf16[6144,128]{1,0:T(8,128)(2,1)} %gate_a.1), channel_id=1, source_target_pairs={{0,1},{1,0},{2,3},{3,2},{4,5},{5,4},{6,7},{7,6},{8,9},{9,8},{10,11... | collective-permute-start | bytes 4718600 | tf_op jit(solution)/shard_map/ppermute | solution.py:247
  20.5 1.9 %collective-permute-start.1 = (bf16[6144,128]{1,0:T(8,128)(2,1)}, bf16[6144,128]{1,0:T(8,128)(2,1)S(1)}, u32[]{:S(2)}, u32[]{:S(2)}) collective-permute-start(bf16[6144,128]{1,0:T(8,128)(2,1)} %up_a.1), channel_id=1, source_target_pairs={{0,1},{1,0},{2,3},{3,2},{4,5},{5,4},{6,7},{7,6},{8,9},{9,8},{10,11... | collective-permute-start | bytes 4718600 | tf_op jit(solution)/shard_map/ppermute | solution.py:248
  22.4 2.4 %collective-permute-start.2 = (bf16[128,6144]{1,0:T(8,128)(2,1)}, bf16[128,6144]{1,0:T(8,128)(2,1)}, u32[]{:S(2)}, u32[]{:S(2)}) collective-permute-start(bf16[128,6144]{1,0:T(8,128)(2,1)} %down_a.1), channel_id=1, source_target_pairs={{0,1},{1,0},{2,3},{3,2},{4,5},{5,4},{6,7},{7,6},{8,9},{9,8},{10,11... | collective-permute-start | bytes 4718600 | tf_op jit(solution)/shard_map/ppermute | solution.py:249
  24.9 1.7 %place.1.place_ref = bf16[3,384,24]{2,1,0:T(8,128)(2,1)} custom-call(s32[2,24]{1,0:T(2,128)} %bitcast.4), custom_call_target="tpu_custom_call" | custom-call | tf_op jit(solution)/shard_map/place/pallas_call | solution.py:250
  26.6 2.9 %all-to-all-done.in_ref = bf16[16,24,128]{2,1,0:T(8,128)(2,1)S(1)} async-done(((bf16[16,24,128]{2,1,0:T(8,128)(2,1)}), bf16[16,24,128]{2,1,0:T(8,128)(2,1)S(1)}, u32[]{:S(2)}, u32[]{:S(2)}) %all-to-all-start) | async-done | bytes 98336 | tf_op jit(solution)/shard_map/all_to_all | solution.py:257
  29.5 0.0 copy-start.1
  29.5 0.0 copy-start.2
  29.5 0.3 repack.1
  29.8 0.0 copy-start
  29.8 0.0 copy-start.4
  29.8 28.7 %all_to_all.20.x_ref = bf16[32,144,128]{2,1,0:T(8,128)(2,1)S(1)} all-to-all(bf16[32,144,128]{2,1,0:T(8,128)(2,1)S(1)} %get-tuple-element.11), channel_id=1, replica_groups=mesh['z'=16,'y'=4,'x'=4,'c'=2] {'y','x','c'}, dimensions={0} | all-to-all | bytes 2359296 | tf_op jit(solution)/shard_map/all_to_all | solution.py:271
  58.5 0.0 collective-permute-done.gate_b
  58.5 0.0 collective-permute-done.1.up_b
  58.5 0.0 collective-permute-done.2.down_b
  58.5 0.0 copy-done.1
  58.5 0.0 copy-done.2
  58.5 0.0 copy-done
  58.6 0.0 copy-done.4
  58.6 3.0 %expert.1 = bf16[32,144,128]{2,1,0:T(8,128)(2,1)S(1)} custom-call(bf16[32,144,128]{2,1,0:T(8,128)(2,1)S(1)} %all_to_all.20.x_ref, f32[96,128]{1,0:T(8,128)S(1)} %get-tuple-element.12.info_ref, bf16[8,6144]{1,0:T(8,128)(2,1)S(1)} %bitcast.2, bf16[6144,128]{1,0:T(8,128)(2,1)S(1)} %copy-done, bf16[6144,128]{1,0:T(8,128)(2,1)S(1)} %collective-permute-done.gate_b, ...), custom_call_target="tpu_custom_call" | custom-call | tf_op jit(solution)/shard_map/expert/pallas_call | solution.py:272
  61.6 0.0 copy-start.3
  61.6 22.6 %all_to_all.21.in_ref = bf16[32,144,128]{2,1,0:T(8,128)(2,1)S(1)} all-to-all(bf16[32,144,128]{2,1,0:T(8,128)(2,1)S(1)} %expert.1), channel_id=1, replica_groups=mesh['z'=16,'y'=4,'x'=4,'c'=2] {'y','x','c'}, dimensions={0} | all-to-all | bytes 2359296 | tf_op jit(solution)/shard_map/all_to_all | solution.py:284
  84.2 0.4 share.1
  84.6 18.0 %all_to_all.22.in_ref = bf16[16,24,128]{2,1,0:T(8,128)(2,1)S(1)} all-to-all(bf16[16,24,128]{2,1,0:T(8,128)(2,1)S(1)} %share.1), channel_id=1, replica_groups=mesh['z'=16,'y'=4,'x'=4,'c'=2] {'z'}, dimensions={0} | all-to-all | bytes 196608 | tf_op jit(solution)/shard_map/all_to_all | solution.py:293
  102.6 0.0 copy-done.3
  102.6 0.9 combine.1
Async XLA Ops:
  1.9 27.6 %all-to-all-start = ((bf16[16,24,128]{2,1,0:T(8,128)(2,1)}), bf16[16,24,128]{2,1,0:T(8,128)(2,1)S(1)}, u32[]{:S(2)}, u32[]{:S(2)}) async-start(bf16[16,24,128]{2,1,0:T(8,128)(2,1)} %dispatch.1), calls=%async_computation | async-start | bytes 196608 | tf_op jit(solution)/shard_map/all_to_all | solution.py:257
  17.6 40.9 %collective-permute-start = (bf16[6144,128]{1,0:T(8,128)(2,1)}, bf16[6144,128]{1,0:T(8,128)(2,1)S(1)}, u32[]{:S(2)}, u32[]{:S(2)}) collective-permute-start(bf16[6144,128]{1,0:T(8,128)(2,1)} %gate_a.1), channel_id=1, source_target_pairs={{0,1},{1,0},{2,3},{3,2},{4,5},{5,4},{6,7},{7,6},{8,9},{9,8},{10,11... | collective-permute-start | bytes 4718600 | tf_op jit(solution)/shard_map/ppermute | solution.py:247
  20.5 38.0 %collective-permute-start.1 = (bf16[6144,128]{1,0:T(8,128)(2,1)}, bf16[6144,128]{1,0:T(8,128)(2,1)S(1)}, u32[]{:S(2)}, u32[]{:S(2)}) collective-permute-start(bf16[6144,128]{1,0:T(8,128)(2,1)} %up_a.1), channel_id=1, source_target_pairs={{0,1},{1,0},{2,3},{3,2},{4,5},{5,4},{6,7},{7,6},{8,9},{9,8},{10,11... | collective-permute-start | bytes 4718600 | tf_op jit(solution)/shard_map/ppermute | solution.py:248
  22.4 36.1 %collective-permute-start.2 = (bf16[128,6144]{1,0:T(8,128)(2,1)}, bf16[128,6144]{1,0:T(8,128)(2,1)}, u32[]{:S(2)}, u32[]{:S(2)}) collective-permute-start(bf16[128,6144]{1,0:T(8,128)(2,1)} %down_a.1), channel_id=1, source_target_pairs={{0,1},{1,0},{2,3},{3,2},{4,5},{5,4},{6,7},{7,6},{8,9},{9,8},{10,11... | collective-permute-start | bytes 4718600 | tf_op jit(solution)/shard_map/ppermute | solution.py:249
  29.5 29.0 %copy-start.1 = (bf16[6144,128]{1,0:T(8,128)(2,1)S(1)}, bf16[6144,128]{1,0:T(8,128)(2,1)}, u32[]{:S(2)}) copy-start(bf16[6144,128]{1,0:T(8,128)(2,1)} %up_a.1) | copy-start | bytes 4718596
  29.5 29.0 %copy-start.2 = (bf16[128,6144]{1,0:T(8,128)(2,1)S(1)}, bf16[128,6144]{1,0:T(8,128)(2,1)}, u32[]{:S(2)}) copy-start(bf16[128,6144]{1,0:T(8,128)(2,1)} %down_a.1) | copy-start | bytes 4718596
  29.8 28.7 %copy-start = (bf16[6144,128]{1,0:T(8,128)(2,1)S(1)}, bf16[6144,128]{1,0:T(8,128)(2,1)}, u32[]{:S(2)}) copy-start(bf16[6144,128]{1,0:T(8,128)(2,1)} %gate_a.1) | copy-start | bytes 4718596
  29.8 28.7 %copy-start.4 = (bf16[6144,8]{0,1:T(8,128)(2,1)S(1)}, bf16[6144,8]{0,1:T(8,128)(2,1)}, u32[]{:S(2)}) copy-start(bf16[6144,8]{0,1:T(8,128)(2,1)} %param.8) | copy-start | bytes 294916
  61.6 41.0 %copy-start.3 = (bf16[3,384,24]{2,1,0:T(8,128)(2,1)S(1)}, bf16[3,384,24]{2,1,0:T(8,128)(2,1)}, u32[]{:S(2)}) copy-start(bf16[3,384,24]{2,1,0:T(8,128)(2,1)} %place.1.place_ref) | copy-start | bytes 165892

commit v4 on v3

--- a/solution.py
+++ b/solution.py
@@ -80,9 +80,10 @@
     return rank_row, i
 
 
-def dispatch_kernel(routes_ref, tok_ref, out_ref):
+def dispatch_kernel(routes_ref, tok_ref, out_ref, rank_ref):
     core = lax.axis_index("c")
     rank_row, i = ranks(routes_ref)
+    rank_ref[...] = rank_row.astype(BF16)
     first = routes_ref[0:1, :]
     second = routes_ref[1:2, :]
     is_a = i < 12
@@ -107,16 +108,6 @@
     payload = payload + dot_nt(onehot(hit_low & (i >= 18)), marks)
     payload = payload + dot_nt(onehot(hit_high & (i >= 18)), marks_high)
     out_ref[...] = payload.reshape(PLANES, PAY, 128).astype(BF16)
-
-
-def place_kernel(routes_ref, out_ref):
-    rank_row, i = ranks(routes_ref)
-    low = rank_row == (i - 12).astype(F32)
-    high = rank_row == (i - 12 + HALF).astype(F32)
-    inside = (i >= 12) & (i < 18)
-    out_ref[0] = onehot((rank_row == i.astype(F32)) & (i < 12))
-    out_ref[1] = onehot(low & inside)
-    out_ref[2] = onehot(high & inside)
 
 
 def repack_kernel(in_ref, out_ref, info_ref):
@@ -222,12 +213,16 @@
     out_ref[...] = spread.reshape(PLANES, PAY, 128).astype(BF16)
 
 
-def combine_kernel(place_ref, in_ref, out_ref):
+def combine_kernel(rank_ref, in_ref, out_ref):
     core = lax.axis_index("c")
     x = in_ref[...].astype(F32).reshape(PAYS, 128).astype(BF16)
-    side = dot_tn(place_ref[0], x)
-    low = dot_tn(place_ref[1], x)
-    high = pltpu.roll(dot_tn(place_ref[2], x), 64, 1)
+    rank = rank_ref[...].astype(F32)
+    i = iota((PLANES, PAY, TOK), 1).reshape(PAYS, TOK)
+    inside = (i >= 12) & (i < 18)
+    side = dot_tn(onehot((rank == i.astype(F32)) & (i < 12)), x)
+    low = dot_tn(onehot((rank == (i - 12).astype(F32)) & inside), x)
+    high = dot_tn(onehot((rank == (i - 12 + HALF).astype(F32)) & inside), x)
+    high = pltpu.roll(high, 64, 1)
     rest = (low + high)[:, :64]
     even = jnp.concatenate([side, rest], axis=1)
     odd = jnp.concatenate([rest, side], axis=1)
@@ -237,23 +232,19 @@
 def local(tokens, routes, w_router, w_gate, w_up, w_down):
     swap = [(0, 1), (1, 0)]
     routes_t = routes.T
-    payload = pl.pallas_call(
+    payload, rank = pl.pallas_call(
         dispatch_kernel,
-        out_shape=jax.ShapeDtypeStruct((PLANES, PAY, 128), BF16),
+        out_shape=(
+            jax.ShapeDtypeStruct((PLANES, PAY, 128), BF16),
+            jax.ShapeDtypeStruct((PAYS, TOK), BF16),
+        ),
         in_specs=[vmem(), vmem()],
-        out_specs=vmem(),
+        out_specs=(vmem(), vmem()),
         name="dispatch",
     )(routes_t, tokens)
     gate_b = lax.ppermute(w_gate, "c", swap)
     up_b = lax.ppermute(w_up, "c", swap)
     down_b = lax.ppermute(w_down, "c", swap)
-    place = pl.pallas_call(
-        place_kernel,
-        out_shape=jax.ShapeDtypeStruct((3, PAYS, TOK), BF16),
-        in_specs=[vmem()],
-        out_specs=vmem(),
-        name="place",
-    )(routes_t)
     arrived = lax.all_to_all(payload, "z", 0, 0, tiled=True)
     blocks, info = pl.pallas_call(
         repack_kernel,
@@ -267,7 +258,6 @@
         cost_estimate=pl.CostEstimate(flops=100000000000, transcendentals=0, bytes_accessed=1048576),
         name="repack",
     )(arrived)
-    blocks, place = lax.optimization_barrier((blocks, place))
     gathered = lax.all_to_all(blocks, ("y", "x", "c"), 0, 0, tiled=True)
     terms = pl.pallas_call(
         expert_kernel,
@@ -298,7 +288,7 @@
         out_specs=vmem(),
         compiler_params=small(),
         name="combine",
-    )(place, back)
+    )(rank, back)
 
 
 def solution(mesh):

time: 104 us -> 103 us (level)
  Pallas kernels: 8.16 us -> 6.44 us
  blocking collectives: 69.3 us -> 67.6 us
  waiting for transfers between devices: 2.94 us -> 4.64 us
    pallas_call x2 -> x1, Pallas kernels: 3.59 us -> 1.88 us  [local(): pl.pallas_call(dispatch_kernel, out_shape=(jax.ShapeDtypeStruct((PLANES,...]
    all_to_all x1, waiting for transfers between devices: 2.94 us -> 4.63 us  [local(): arrived = lax.all_to_all(payload, 'z', 0, 0, tiled=True)]
    all_to_all x1, blocking collectives: 18 us -> 16.3 us  [local(): back = lax.all_to_all(shares, 'z', 0, 0, tiled=True)]
  transfers between devices with their start and end apart: 4 -> 4, of which waited for: 1 -> 1; matrix products, arithmetic and copies ran while one was open for 0% -> 0% of each run, Pallas kernels for 2% -> 0%
where the time goes in v4:
time: 103 us; the launch traced here: 102 us
  blocking collectives  67.6 us (66%)
  starting transfers between devices  22.9 us (22%)
  Pallas kernels  6.44 us (6%)
  waiting for transfers between devices  4.64 us (5%)
    all_to_all x1, blocking collectives, local(): gathered = lax.all_to_all(blocks, ('y', 'x', 'c'), 0, 0, tiled=True)  28.7 us
    all_to_all x1, blocking collectives, local(): parts = lax.all_to_all(terms, ('y', 'x', 'c'), 0, 0, tiled=True)  22.6 us
    all_to_all x1, blocking collectives, local(): back = lax.all_to_all(shares, 'z', 0, 0, tiled=True)  16.3 us
    all_to_all x1, starting transfers between devices, local(): arrived = lax.all_to_all(payload, 'z', 0, 0, tiled=True)  15.7 us
    all_to_all x1, waiting for transfers between devices, local(): arrived = lax.all_to_all(payload, 'z', 0, 0, tiled=True)  4.63 us
    pallas_call x1, Pallas kernels, local(): pl.pallas_call(expert_kernel, out_shape=jax.ShapeDtypeStruct((2 * CHIPS,...  2.99 us
    ppermute x1, starting transfers between devices, local(): gate_b = lax.ppermute(w_gate, 'c', swap)  2.87 us
    ppermute x1, starting transfers between devices, local(): down_b = lax.ppermute(w_down, 'c', swap)  2.41 us
  transfers between devices with their start and end apart: 4, of which 1 were waited for; matrix products, arithmetic and copies ran while one was open for 0% of the time, Pallas kernels for 0%

profile of v4, /device:TPU:1, one launch (start us, length us, event | category | flops | bytes accessed | tf_op | source)
XLA Modules:
  0.0 101.8 jit_solution(13154718505002365769)
XLA Ops:
  0.0 1.9 %dispatch.1 = (bf16[16,24,128]{2,1,0:T(8,128)(2,1)}, bf16[384,24]{1,0:T(8,128)(2,1)}) custom-call(s32[2,24]{1,0:T(2,128)} %bitcast.3, bf16[24,192]{1,0:T(8,128)(2,1)} %tok_ref.1), custom_call_target="tpu_custom_call" | custom-call | tf_op jit(solution)/shard_map/dispatch/pallas_call | solution.py:235
  1.9 15.7 %all-to-all-start = ((bf16[16,24,128]{2,1,0:T(8,128)(2,1)}), bf16[16,24,128]{2,1,0:T(8,128)(2,1)S(1)}, u32[]{:S(2)}, u32[]{:S(2)}) async-start(bf16[16,24,128]{2,1,0:T(8,128)(2,1)} %get-tuple-element.10), calls=%async_computation | async-start | bytes 196608 | tf_op jit(solution)/shard_map/all_to_all | solution.py:248
  17.6 2.9 %collective-permute-start = (bf16[6144,128]{1,0:T(8,128)(2,1)}, bf16[6144,128]{1,0:T(8,128)(2,1)S(1)}, u32[]{:S(2)}, u32[]{:S(2)}) collective-permute-start(bf16[6144,128]{1,0:T(8,128)(2,1)} %gate_a.1), channel_id=1, source_target_pairs={{0,1},{1,0},{2,3},{3,2},{4,5},{5,4},{6,7},{7,6},{8,9},{9,8},{10,11... | collective-permute-start | bytes 4718600 | tf_op jit(solution)/shard_map/ppermute | solution.py:245
  20.5 1.9 %collective-permute-start.1 = (bf16[6144,128]{1,0:T(8,128)(2,1)}, bf16[6144,128]{1,0:T(8,128)(2,1)S(1)}, u32[]{:S(2)}, u32[]{:S(2)}) collective-permute-start(bf16[6144,128]{1,0:T(8,128)(2,1)} %up_a.1), channel_id=1, source_target_pairs={{0,1},{1,0},{2,3},{3,2},{4,5},{5,4},{6,7},{7,6},{8,9},{9,8},{10,11... | collective-permute-start | bytes 4718600 | tf_op jit(solution)/shard_map/ppermute | solution.py:246
  22.4 2.4 %collective-permute-start.2 = (bf16[128,6144]{1,0:T(8,128)(2,1)}, bf16[128,6144]{1,0:T(8,128)(2,1)}, u32[]{:S(2)}, u32[]{:S(2)}) collective-permute-start(bf16[128,6144]{1,0:T(8,128)(2,1)} %down_a.1), channel_id=1, source_target_pairs={{0,1},{1,0},{2,3},{3,2},{4,5},{5,4},{6,7},{7,6},{8,9},{9,8},{10,11... | collective-permute-start | bytes 4718600 | tf_op jit(solution)/shard_map/ppermute | solution.py:247
  24.9 4.6 %all-to-all-done.in_ref = bf16[16,24,128]{2,1,0:T(8,128)(2,1)S(1)} async-done(((bf16[16,24,128]{2,1,0:T(8,128)(2,1)}), bf16[16,24,128]{2,1,0:T(8,128)(2,1)S(1)}, u32[]{:S(2)}, u32[]{:S(2)}) %all-to-all-start) | async-done | bytes 98336 | tf_op jit(solution)/shard_map/all_to_all | solution.py:248
  29.5 0.0 copy-start.1
  29.5 0.0 copy-start.2
  29.5 0.3 repack.1
  29.8 0.0 copy-start
  29.8 0.0 copy-start.3
  29.8 28.7 %all_to_all.20.x_ref = bf16[32,144,128]{2,1,0:T(8,128)(2,1)S(1)} all-to-all(bf16[32,144,128]{2,1,0:T(8,128)(2,1)S(1)} %get-tuple-element.11), channel_id=1, replica_groups=mesh['z'=16,'y'=4,'x'=4,'c'=2] {'y','x','c'}, dimensions={0} | all-to-all | bytes 2359296 | tf_op jit(solution)/shard_map/all_to_all | solution.py:261
  58.5 0.0 collective-permute-done.gate_b
  58.5 0.0 collective-permute-done.1.up_b
  58.5 0.0 collective-permute-done.2.down_b
  58.5 0.0 copy-done.1
  58.5 0.0 copy-done.2
  58.5 0.0 copy-done
  58.6 0.0 copy-done.3
  58.6 3.0 %expert.1 = bf16[32,144,128]{2,1,0:T(8,128)(2,1)S(1)} custom-call(bf16[32,144,128]{2,1,0:T(8,128)(2,1)S(1)} %all_to_all.20.x_ref, f32[96,128]{1,0:T(8,128)S(1)} %get-tuple-element.12.info_ref, bf16[8,6144]{1,0:T(8,128)(2,1)S(1)} %bitcast.2, bf16[6144,128]{1,0:T(8,128)(2,1)S(1)} %copy-done, bf16[6144,128]{1,0:T(8,128)(2,1)S(1)} %collective-permute-done.gate_b, ...), custom_call_target="tpu_custom_call" | custom-call | tf_op jit(solution)/shard_map/expert/pallas_call | solution.py:262
  61.6 0.0 copy-start.4
  61.6 22.6 %all_to_all.21.in_ref = bf16[32,144,128]{2,1,0:T(8,128)(2,1)S(1)} all-to-all(bf16[32,144,128]{2,1,0:T(8,128)(2,1)S(1)} %expert.1), channel_id=1, replica_groups=mesh['z'=16,'y'=4,'x'=4,'c'=2] {'y','x','c'}, dimensions={0} | all-to-all | bytes 2359296 | tf_op jit(solution)/shard_map/all_to_all | solution.py:274
  84.2 0.4 share.1
  84.6 16.3 %all_to_all.22.in_ref = bf16[16,24,128]{2,1,0:T(8,128)(2,1)S(1)} all-to-all(bf16[16,24,128]{2,1,0:T(8,128)(2,1)S(1)} %share.1), channel_id=1, replica_groups=mesh['z'=16,'y'=4,'x'=4,'c'=2] {'z'}, dimensions={0} | all-to-all | bytes 196608 | tf_op jit(solution)/shard_map/all_to_all | solution.py:283
  100.9 0.0 copy-done.4
  100.9 0.9 combine.1
Async XLA Ops:
  1.9 27.6 %all-to-all-start = ((bf16[16,24,128]{2,1,0:T(8,128)(2,1)}), bf16[16,24,128]{2,1,0:T(8,128)(2,1)S(1)}, u32[]{:S(2)}, u32[]{:S(2)}) async-start(bf16[16,24,128]{2,1,0:T(8,128)(2,1)} %get-tuple-element.10), calls=%async_computation | async-start | bytes 196608 | tf_op jit(solution)/shard_map/all_to_all | solution.py:248
  17.6 40.9 %collective-permute-start = (bf16[6144,128]{1,0:T(8,128)(2,1)}, bf16[6144,128]{1,0:T(8,128)(2,1)S(1)}, u32[]{:S(2)}, u32[]{:S(2)}) collective-permute-start(bf16[6144,128]{1,0:T(8,128)(2,1)} %gate_a.1), channel_id=1, source_target_pairs={{0,1},{1,0},{2,3},{3,2},{4,5},{5,4},{6,7},{7,6},{8,9},{9,8},{10,11... | collective-permute-start | bytes 4718600 | tf_op jit(solution)/shard_map/ppermute | solution.py:245
  20.5 38.0 %collective-permute-start.1 = (bf16[6144,128]{1,0:T(8,128)(2,1)}, bf16[6144,128]{1,0:T(8,128)(2,1)S(1)}, u32[]{:S(2)}, u32[]{:S(2)}) collective-permute-start(bf16[6144,128]{1,0:T(8,128)(2,1)} %up_a.1), channel_id=1, source_target_pairs={{0,1},{1,0},{2,3},{3,2},{4,5},{5,4},{6,7},{7,6},{8,9},{9,8},{10,11... | collective-permute-start | bytes 4718600 | tf_op jit(solution)/shard_map/ppermute | solution.py:246
  22.4 36.1 %collective-permute-start.2 = (bf16[128,6144]{1,0:T(8,128)(2,1)}, bf16[128,6144]{1,0:T(8,128)(2,1)}, u32[]{:S(2)}, u32[]{:S(2)}) collective-permute-start(bf16[128,6144]{1,0:T(8,128)(2,1)} %down_a.1), channel_id=1, source_target_pairs={{0,1},{1,0},{2,3},{3,2},{4,5},{5,4},{6,7},{7,6},{8,9},{9,8},{10,11... | collective-permute-start | bytes 4718600 | tf_op jit(solution)/shard_map/ppermute | solution.py:247
  29.5 29.0 %copy-start.1 = (bf16[6144,128]{1,0:T(8,128)(2,1)S(1)}, bf16[6144,128]{1,0:T(8,128)(2,1)}, u32[]{:S(2)}) copy-start(bf16[6144,128]{1,0:T(8,128)(2,1)} %up_a.1) | copy-start | bytes 4718596
  29.5 29.0 %copy-start.2 = (bf16[128,6144]{1,0:T(8,128)(2,1)S(1)}, bf16[128,6144]{1,0:T(8,128)(2,1)}, u32[]{:S(2)}) copy-start(bf16[128,6144]{1,0:T(8,128)(2,1)} %down_a.1) | copy-start | bytes 4718596
  29.8 28.7 %copy-start = (bf16[6144,128]{1,0:T(8,128)(2,1)S(1)}, bf16[6144,128]{1,0:T(8,128)(2,1)}, u32[]{:S(2)}) copy-start(bf16[6144,128]{1,0:T(8,128)(2,1)} %gate_a.1) | copy-start | bytes 4718596
  29.8 28.7 %copy-start.3 = (bf16[6144,8]{0,1:T(8,128)(2,1)S(1)}, bf16[6144,8]{0,1:T(8,128)(2,1)}, u32[]{:S(2)}) copy-start(bf16[6144,8]{0,1:T(8,128)(2,1)} %param.8) | copy-start | bytes 294916
  61.6 39.3 %copy-start.4 = (bf16[384,24]{1,0:T(8,128)(2,1)S(1)}, bf16[384,24]{1,0:T(8,128)(2,1)}, u32[]{:S(2)}) copy-start(bf16[384,24]{1,0:T(8,128)(2,1)} %get-tuple-element.9.rank_ref) | copy-start | bytes 55300

commit v5 on v4

--- a/solution.py
+++ b/solution.py
@@ -14,8 +14,10 @@
 FEAT = 192
 PAIR = 384
 D = 6144
-PAY = 24
+PAY = 20
 PAYS = PLANES * PAY
+BACK = 18
+BACKS = PLANES * BACK
 UNITS = 256
 PACK = ROWS + ROWS // 2
 PER = 16
@@ -72,25 +74,18 @@
     named = onehot((k8 == first) | (k8 == second))
     earlier = onehot(iota((TOK, TOK), 0) < iota((TOK, TOK), 1))
     rank = dot_nn(named, earlier)
-    rank = jnp.where(named.astype(F32) > 0.5, rank, 100.0).astype(BF16)
-    plane = iota((PLANES, PAY, EXPERTS), 0).reshape(PAYS, EXPERTS)
-    pick = onehot((plane >> 1) == iota((PAYS, EXPERTS), 1))
-    rank_row = dot_nn(pick, rank)
-    i = iota((PLANES, PAY, TOK), 1).reshape(PAYS, TOK)
-    return rank_row, i
+    return jnp.where(named.astype(F32) > 0.5, rank, 100.0).astype(BF16)
 
 
 def dispatch_kernel(routes_ref, tok_ref, out_ref, rank_ref):
     core = lax.axis_index("c")
-    rank_row, i = ranks(routes_ref)
-    rank_ref[...] = rank_row.astype(BF16)
-    first = routes_ref[0:1, :]
-    second = routes_ref[1:2, :]
-    is_a = i < 12
-    is_b = (i >= 12) & (i < 18)
-    slot = jnp.where(is_a, i, jnp.where(is_b, i - 12, i - 18))
-    hit_low = rank_row == slot.astype(F32)
-    hit_high = (rank_row == (slot + HALF).astype(F32)) & (i >= 12)
+    rank = ranks(routes_ref)
+    row = iota((PAYS, EXPERTS), 0)
+    plane = (row * 205) >> 12
+    mine = (plane >> 1) == iota((PAYS, EXPERTS), 1)
+    rank_row = dot_nn(onehot(mine), rank)
+    row = iota((PAYS, TOK), 0)
+    i = row - PAY * ((row * 205) >> 12)
     tok = tok_ref[...].astype(F32)
     zero = jnp.zeros((TOK, 64), F32)
     part_a = jnp.where(core == 0, tok[:, :128], tok[:, 64:]).astype(BF16)
@@ -99,22 +94,38 @@
     part_b = jnp.where(core == 0, tail, head)
     part_b_high = pltpu.roll(part_b, 64, 1).astype(BF16)
     part_b = part_b.astype(BF16)
-    lane = iota((128, TOK), 0)
-    marks = onehot((lane == first) | (lane == second))
-    marks_high = onehot((lane - 64 == first) | (lane - 64 == second))
-    payload = dot_nn(onehot(hit_low & is_a), part_a)
-    payload = payload + dot_nn(onehot(hit_low & is_b), part_b)
-    payload = payload + dot_nn(onehot(hit_high & is_b), part_b_high)
-    payload = payload + dot_nt(onehot(hit_low & (i >= 18)), marks)
-    payload = payload + dot_nt(onehot(hit_high & (i >= 18)), marks_high)
-    out_ref[...] = payload.reshape(PLANES, PAY, 128).astype(BF16)
+    payload = dot_nn(onehot((rank_row == i.astype(F32)) & (i < 12)), part_a)
+    rest = (i >= 12) & (i < 18)
+    payload = payload + dot_nn(onehot((rank_row == (i - 12).astype(F32)) & rest), part_b)
+    rest_high = (rank_row == (i - 12 + HALF).astype(F32)) & rest
+    payload = payload + dot_nn(onehot(rest_high), part_b_high)
+    first = routes_ref[0:1, :]
+    second = routes_ref[1:2, :]
+    k8 = iota((EXPERTS, TOK), 0)
+    named = onehot((k8 == first) | (k8 == second))
+    lane = iota((EXPERTS, 128), 1)
+    named_lane = dot_tn(named, onehot((lane & 7) == iota((EXPERTS, 128), 0)))
+    rank_col = dot_tn(rank, onehot(iota((EXPERTS, EXPERTS), 0) == iota((EXPERTS, EXPERTS), 1)))
+    slot = (iota((TOK, 128), 1) >> 3).astype(F32)
+    marks = [
+        jnp.sum(jnp.where(rank_col[:, k : k + 1] == slot, named_lane, 0.0), axis=0, keepdims=True)
+        for k in range(EXPERTS)
+    ]
+    marks = jnp.concatenate(marks, axis=0).astype(BF16)
+    at = iota((PAYS, EXPERTS), 0) - PAY * plane
+    payload = payload + dot_nn(onehot(mine & (at == 18)), marks)
+    out_ref[...] = payload.astype(BF16)
+    plane = (iota((BACKS, EXPERTS), 0) * 57) >> 10
+    rank_ref[...] = dot_nn(onehot((plane >> 1) == iota((BACKS, EXPERTS), 1)), rank).astype(BF16)
 
 
 def repack_kernel(in_ref, out_ref, info_ref):
     core = lax.axis_index("c")
-    x = in_ref[...].astype(F32).reshape(PAYS, 128).astype(BF16)
+    x = in_ref[...]
     p = iota((ROWS, PAYS), 0)
-    at = iota((ROWS, PAYS), 1) - p - (PAY - HALF) * ((p * 43) >> 8)
+    home = (p * 43) >> 8
+    col = iota((ROWS, PAYS), 1)
+    at = col - p - (PAY - HALF) * home
     rest = dot_nn(onehot(at == 12), x)
     near = rest[: ROWS // 2]
     far = rest[ROWS // 2 :]
@@ -134,8 +145,11 @@
         out_ref[2 * chip, ROWS:] = even_rest
         out_ref[2 * chip + 1, :ROWS] = odd
         out_ref[2 * chip + 1, ROWS:] = odd_rest
-    info = dot_nn(onehot(at == 18), x)
-    info_ref[...] = jnp.where(core == 0, info, pltpu.roll(info, 64, 1))
+    marks = dot_nn(onehot(col - PAY * home == 18), x)
+    p = iota((ROWS, 128), 0)
+    slot = p - HALF * ((p * 43) >> 8) + HALF * core
+    marks = jnp.where((iota((ROWS, 128), 1) >> 3) == slot, marks, 0.0).astype(BF16)
+    info_ref[...] = dot_nn(marks, onehot((iota((128, 128), 0) & 7) == iota((128, 128), 1)))
 
 
 def expert_kernel(
@@ -205,23 +219,23 @@
     near = jnp.where(core == 0, low, high)
     far = jnp.where(core == 0, high, low)
     rest = jnp.concatenate([near, far], axis=0).astype(BF16)
-    p = iota((PAYS, ROWS), 1)
-    at = iota((PAYS, ROWS), 0) - p - (PAY - HALF) * ((p * 43) >> 8)
+    p = iota((BACKS, ROWS), 1)
+    at = iota((BACKS, ROWS), 0) - p - (BACK - HALF) * ((p * 43) >> 8)
     spread = dot_nn(onehot(at == 0), halves[0][:ROWS].astype(BF16))
     spread = spread + dot_nn(onehot(at == HALF), halves[1][:ROWS].astype(BF16))
     spread = spread + dot_nn(onehot(at == 2 * HALF), rest)
-    out_ref[...] = spread.reshape(PLANES, PAY, 128).astype(BF16)
+    out_ref[...] = spread.astype(BF16)
 
 
 def combine_kernel(rank_ref, in_ref, out_ref):
     core = lax.axis_index("c")
-    x = in_ref[...].astype(F32).reshape(PAYS, 128).astype(BF16)
+    x = in_ref[...]
     rank = rank_ref[...].astype(F32)
-    i = iota((PLANES, PAY, TOK), 1).reshape(PAYS, TOK)
-    inside = (i >= 12) & (i < 18)
+    row = iota((BACKS, TOK), 0)
+    i = row - BACK * ((row * 57) >> 10)
     side = dot_tn(onehot((rank == i.astype(F32)) & (i < 12)), x)
-    low = dot_tn(onehot((rank == (i - 12).astype(F32)) & inside), x)
-    high = dot_tn(onehot((rank == (i - 12 + HALF).astype(F32)) & inside), x)
+    low = dot_tn(onehot((rank == (i - 12).astype(F32)) & (i >= 12)), x)
+    high = dot_tn(onehot((rank == (i - 12 + HALF).astype(F32)) & (i >= 12)), x)
     high = pltpu.roll(high, 64, 1)
     rest = (low + high)[:, :64]
     even = jnp.concatenate([side, rest], axis=1)
@@ -235,8 +249,8 @@
     payload, rank = pl.pallas_call(
         dispatch_kernel,
         out_shape=(
-            jax.ShapeDtypeStruct((PLANES, PAY, 128), BF16),
-            jax.ShapeDtypeStruct((PAYS, TOK), BF16),
+            jax.ShapeDtypeStruct((PAYS, 128), BF16),
+            jax.ShapeDtypeStruct((BACKS, TOK), BF16),
         ),
         in_specs=[vmem(), vmem()],
         out_specs=(vmem(), vmem()),
@@ -245,7 +259,8 @@
     gate_b = lax.ppermute(w_gate, "c", swap)
     up_b = lax.ppermute(w_up, "c", swap)
     down_b = lax.ppermute(w_down, "c", swap)
-    arrived = lax.all_to_all(payload, "z", 0, 0, tiled=True)
+    payload = payload.reshape(PLANES, PAY // 2, 2, 128)
+    arrived = lax.all_to_all(payload, "z", 0, 0, tiled=True).reshape(PAYS, 128)
     blocks, info = pl.pallas_call(
         repack_kernel,
         out_shape=(
@@ -274,13 +289,14 @@
     parts = lax.all_to_all(terms, ("y", "x", "c"), 0, 0, tiled=True)
     shares = pl.pallas_call(
         share_kernel,
-        out_shape=jax.ShapeDtypeStruct((PLANES, PAY, 128), BF16),
+        out_shape=jax.ShapeDtypeStruct((BACKS, 128), BF16),
         in_specs=[vmem()],
         out_specs=vmem(),
         compiler_params=small(),
         name="share",
     )(parts)
-    back = lax.all_to_all(shares, "z", 0, 0, tiled=True)
+    shares = shares.reshape(PLANES, BACK // 2, 2, 128)
+    back = lax.all_to_all(shares, "z", 0, 0, tiled=True).reshape(BACKS, 128)
     return pl.pallas_call(
         combine_kernel,
         out_shape=jax.ShapeDtypeStruct((TOK, FEAT), BF16),

time: 103 us -> 102 us (level); the launches traced: 102 us -> 102 us
  no operation moved by 1% of the time
where the time goes in v5:
time: 102 us
  blocking collectives  67.5 us (66%)
  starting transfers between devices  22.9 us (22%)
  Pallas kernels  6.69 us (7%)
  waiting for transfers between devices  4.57 us (4%)
    all_to_all x1, blocking collectives, local(): gathered = lax.all_to_all(blocks, ('y', 'x', 'c'), 0, 0, tiled=True)  28.4 us
    all_to_all x1, blocking collectives, local(): parts = lax.all_to_all(terms, ('y', 'x', 'c'), 0, 0, tiled=True)  22.7 us
    all_to_all x1, blocking collectives, local(): back = lax.all_to_all(shares, 'z', 0, 0, tiled=True).reshape(BACKS, 128)  16.4 us
    all_to_all x1, starting transfers between devices, local(): arrived = lax.all_to_all(payload, 'z', 0, 0, tiled=True).reshape(PAYS, 128)  15.7 us
    all_to_all x1, waiting for transfers between devices, local(): arrived = lax.all_to_all(payload, 'z', 0, 0, tiled=True).reshape(PAYS, 128)  4.56 us
    pallas_call x1, Pallas kernels, local(): pl.pallas_call(expert_kernel, out_shape=jax.ShapeDtypeStruct((2 * CHIPS,...  3 us
    ppermute x1, starting transfers between devices, local(): gate_b = lax.ppermute(w_gate, 'c', swap)  2.87 us
    ppermute x1, starting transfers between devices, local(): down_b = lax.ppermute(w_down, 'c', swap)  2.41 us
  transfers between devices with their start and end apart: 4, of which 1 were waited for; matrix products, arithmetic and copies ran while one was open for 0% of the time, Pallas kernels for 0%

profile of v5, /device:TPU:1, one launch (start us, length us, event | category | flops | bytes accessed | tf_op | source)
XLA Modules:
  0.0 101.8 jit_solution(11879557181138162672)
XLA Ops:
  0.0 2.1 %dispatch.1 = (bf16[320,128]{1,0:T(8,128)(2,1)}, bf16[288,24]{1,0:T(8,128)(2,1)}) custom-call(s32[2,24]{1,0:T(2,128)} %bitcast.11, bf16[24,192]{1,0:T(8,128)(2,1)} %tok_ref.1), custom_call_target="tpu_custom_call" | custom-call | tf_op jit(solution)/shard_map/dispatch/pallas_call | solution.py:249
  2.1 15.7 %all-to-all-start = ((bf16[16,10,2,128]{3,2,1,0:T(2,128)(2,1)}), bf16[16,10,2,128]{3,2,1,0:T(2,128)(2,1)S(1)}, u32[]{:S(2)}, u32[]{:S(2)}) async-start(bf16[16,10,2,128]{3,2,1,0:T(2,128)(2,1)} %bitcast.10), calls=%async_computation | async-start | bytes 163840 | tf_op jit(solution)/shard_map/all_to_all | solution.py:263
  17.8 2.9 %collective-permute-start = (bf16[6144,128]{1,0:T(8,128)(2,1)}, bf16[6144,128]{1,0:T(8,128)(2,1)S(1)}, u32[]{:S(2)}, u32[]{:S(2)}) collective-permute-start(bf16[6144,128]{1,0:T(8,128)(2,1)} %gate_a.1), channel_id=1, source_target_pairs={{0,1},{1,0},{2,3},{3,2},{4,5},{5,4},{6,7},{7,6},{8,9},{9,8},{10,11... | collective-permute-start | bytes 4718600 | tf_op jit(solution)/shard_map/ppermute | solution.py:259
  20.7 1.9 %collective-permute-start.1 = (bf16[6144,128]{1,0:T(8,128)(2,1)}, bf16[6144,128]{1,0:T(8,128)(2,1)S(1)}, u32[]{:S(2)}, u32[]{:S(2)}) collective-permute-start(bf16[6144,128]{1,0:T(8,128)(2,1)} %up_a.1), channel_id=1, source_target_pairs={{0,1},{1,0},{2,3},{3,2},{4,5},{5,4},{6,7},{7,6},{8,9},{9,8},{10,11... | collective-permute-start | bytes 4718600 | tf_op jit(solution)/shard_map/ppermute | solution.py:260
  22.6 2.4 %collective-permute-start.2 = (bf16[128,6144]{1,0:T(8,128)(2,1)}, bf16[128,6144]{1,0:T(8,128)(2,1)}, u32[]{:S(2)}, u32[]{:S(2)}) collective-permute-start(bf16[128,6144]{1,0:T(8,128)(2,1)} %down_a.1), channel_id=1, source_target_pairs={{0,1},{1,0},{2,3},{3,2},{4,5},{5,4},{6,7},{7,6},{8,9},{9,8},{10,11... | collective-permute-start | bytes 4718600 | tf_op jit(solution)/shard_map/ppermute | solution.py:261
  25.0 4.6 %all-to-all-done = bf16[16,10,2,128]{3,2,1,0:T(2,128)(2,1)S(1)} async-done(((bf16[16,10,2,128]{3,2,1,0:T(2,128)(2,1)}), bf16[16,10,2,128]{3,2,1,0:T(2,128)(2,1)S(1)}, u32[]{:S(2)}, u32[]{:S(2)}) %all-to-all-start) | async-done | bytes 81952 | tf_op jit(solution)/shard_map/all_to_all | solution.py:263
  29.6 0.0 copy-start.1
  29.6 0.0 copy-start.2
  29.6 0.3 repack.1
  30.0 0.0 copy-start
  30.0 0.0 copy-start.3
  30.0 28.4 %all_to_all.20.x_ref = bf16[32,144,128]{2,1,0:T(8,128)(2,1)S(1)} all-to-all(bf16[32,144,128]{2,1,0:T(8,128)(2,1)S(1)} %get-tuple-element.11), channel_id=1, replica_groups=mesh['z'=16,'y'=4,'x'=4,'c'=2] {'y','x','c'}, dimensions={0} | all-to-all | bytes 2359296 | tf_op jit(solution)/shard_map/all_to_all | solution.py:276
  58.3 0.0 collective-permute-done.gate_b
  58.3 0.0 collective-permute-done.1.up_b
  58.4 0.0 collective-permute-done.2.down_b
  58.4 0.0 copy-done.1
  58.4 0.0 copy-done.2
  58.4 0.0 copy-done
  58.4 0.0 copy-done.3
  58.4 3.0 %expert.1 = bf16[32,144,128]{2,1,0:T(8,128)(2,1)S(1)} custom-call(bf16[32,144,128]{2,1,0:T(8,128)(2,1)S(1)} %all_to_all.20.x_ref, f32[96,128]{1,0:T(8,128)S(1)} %get-tuple-element.12.info_ref, bf16[8,6144]{1,0:T(8,128)(2,1)S(1)} %bitcast.8, bf16[6144,128]{1,0:T(8,128)(2,1)S(1)} %copy-done, bf16[6144,128]{1,0:T(8,128)(2,1)S(1)} %collective-permute-done.gate_b, ...), custom_call_target="tpu_custom_call" | custom-call | tf_op jit(solution)/shard_map/expert/pallas_call | solution.py:277
  61.4 0.0 copy-start.4
  61.4 22.7 %all_to_all.21.in_ref = bf16[32,144,128]{2,1,0:T(8,128)(2,1)S(1)} all-to-all(bf16[32,144,128]{2,1,0:T(8,128)(2,1)S(1)} %expert.1), channel_id=1, replica_groups=mesh['z'=16,'y'=4,'x'=4,'c'=2] {'y','x','c'}, dimensions={0} | all-to-all | bytes 2359296 | tf_op jit(solution)/shard_map/all_to_all | solution.py:289
  84.1 0.4 share.1
  84.4 16.4 %all_to_all.22 = bf16[16,9,2,128]{3,2,1,0:T(2,128)(2,1)S(1)} all-to-all(bf16[16,9,2,128]{3,2,1,0:T(2,128)(2,1)S(1)} %bitcast.6), channel_id=1, replica_groups=mesh['z'=16,'y'=4,'x'=4,'c'=2] {'z'}, dimensions={0} | all-to-all | bytes 147456 | tf_op jit(solution)/shard_map/all_to_all | solution.py:299
  100.9 0.0 copy-done.4
  100.9 0.9 combine.1
Async XLA Ops:
  2.1 27.5 %all-to-all-start = ((bf16[16,10,2,128]{3,2,1,0:T(2,128)(2,1)}), bf16[16,10,2,128]{3,2,1,0:T(2,128)(2,1)S(1)}, u32[]{:S(2)}, u32[]{:S(2)}) async-start(bf16[16,10,2,128]{3,2,1,0:T(2,128)(2,1)} %bitcast.10), calls=%async_computation | async-start | bytes 163840 | tf_op jit(solution)/shard_map/all_to_all | solution.py:263
  17.8 40.5 %collective-permute-start = (bf16[6144,128]{1,0:T(8,128)(2,1)}, bf16[6144,128]{1,0:T(8,128)(2,1)S(1)}, u32[]{:S(2)}, u32[]{:S(2)}) collective-permute-start(bf16[6144,128]{1,0:T(8,128)(2,1)} %gate_a.1), channel_id=1, source_target_pairs={{0,1},{1,0},{2,3},{3,2},{4,5},{5,4},{6,7},{7,6},{8,9},{9,8},{10,11... | collective-permute-start | bytes 4718600 | tf_op jit(solution)/shard_map/ppermute | solution.py:259
  20.7 37.7 %collective-permute-start.1 = (bf16[6144,128]{1,0:T(8,128)(2,1)}, bf16[6144,128]{1,0:T(8,128)(2,1)S(1)}, u32[]{:S(2)}, u32[]{:S(2)}) collective-permute-start(bf16[6144,128]{1,0:T(8,128)(2,1)} %up_a.1), channel_id=1, source_target_pairs={{0,1},{1,0},{2,3},{3,2},{4,5},{5,4},{6,7},{7,6},{8,9},{9,8},{10,11... | collective-permute-start | bytes 4718600 | tf_op jit(solution)/shard_map/ppermute | solution.py:260
  22.6 35.7 %collective-permute-start.2 = (bf16[128,6144]{1,0:T(8,128)(2,1)}, bf16[128,6144]{1,0:T(8,128)(2,1)}, u32[]{:S(2)}, u32[]{:S(2)}) collective-permute-start(bf16[128,6144]{1,0:T(8,128)(2,1)} %down_a.1), channel_id=1, source_target_pairs={{0,1},{1,0},{2,3},{3,2},{4,5},{5,4},{6,7},{7,6},{8,9},{9,8},{10,11... | collective-permute-start | bytes 4718600 | tf_op jit(solution)/shard_map/ppermute | solution.py:261
  29.6 28.8 %copy-start.1 = (bf16[6144,128]{1,0:T(8,128)(2,1)S(1)}, bf16[6144,128]{1,0:T(8,128)(2,1)}, u32[]{:S(2)}) copy-start(bf16[6144,128]{1,0:T(8,128)(2,1)} %up_a.1) | copy-start | bytes 4718596
  29.6 28.8 %copy-start.2 = (bf16[128,6144]{1,0:T(8,128)(2,1)S(1)}, bf16[128,6144]{1,0:T(8,128)(2,1)}, u32[]{:S(2)}) copy-start(bf16[128,6144]{1,0:T(8,128)(2,1)} %down_a.1) | copy-start | bytes 4718596
  30.0 28.4 %copy-start = (bf16[6144,128]{1,0:T(8,128)(2,1)S(1)}, bf16[6144,128]{1,0:T(8,128)(2,1)}, u32[]{:S(2)}) copy-start(bf16[6144,128]{1,0:T(8,128)(2,1)} %gate_a.1) | copy-start | bytes 4718596
  30.0 28.4 %copy-start.3 = (bf16[6144,8]{0,1:T(8,128)(2,1)S(1)}, bf16[6144,8]{0,1:T(8,128)(2,1)}, u32[]{:S(2)}) copy-start(bf16[6144,8]{0,1:T(8,128)(2,1)} %param.8) | copy-start | bytes 294916
  61.4 39.5 %copy-start.4 = (bf16[288,24]{1,0:T(8,128)(2,1)S(1)}, bf16[288,24]{1,0:T(8,128)(2,1)}, u32[]{:S(2)}) copy-start(bf16[288,24]{1,0:T(8,128)(2,1)} %get-tuple-element.9.rank_ref) | copy-start | bytes 41476

commit v6 on v5

--- a/solution.py
+++ b/solution.py
@@ -31,16 +31,8 @@
     return pl.BlockSpec(memory_space=pltpu.VMEM)
 
 
-def smem():
-    return pl.BlockSpec(memory_space=pltpu.SMEM)
-
-
 def hbm():
     return pl.BlockSpec(memory_space=pltpu.HBM)
-
-
-def anyspace():
-    return pl.BlockSpec(memory_space=pl.ANY)
 
 
 def small():
@@ -115,8 +107,9 @@
     at = iota((PAYS, EXPERTS), 0) - PAY * plane
     payload = payload + dot_nn(onehot(mine & (at == 18)), marks)
     out_ref[...] = payload.astype(BF16)
-    plane = (iota((BACKS, EXPERTS), 0) * 57) >> 10
-    rank_ref[...] = dot_nn(onehot((plane >> 1) == iota((BACKS, EXPERTS), 1)), rank).astype(BF16)
+    plane = (iota((EXPERTS, BACKS), 1) * 57) >> 10
+    pick = onehot((plane >> 1) == iota((EXPERTS, BACKS), 0))
+    rank_ref[...] = dot_tn(rank, pick).astype(BF16)
 
 
 def repack_kernel(in_ref, out_ref, info_ref):
@@ -231,11 +224,11 @@
     core = lax.axis_index("c")
     x = in_ref[...]
     rank = rank_ref[...].astype(F32)
-    row = iota((BACKS, TOK), 0)
+    row = iota((TOK, BACKS), 1)
     i = row - BACK * ((row * 57) >> 10)
-    side = dot_tn(onehot((rank == i.astype(F32)) & (i < 12)), x)
-    low = dot_tn(onehot((rank == (i - 12).astype(F32)) & (i >= 12)), x)
-    high = dot_tn(onehot((rank == (i - 12 + HALF).astype(F32)) & (i >= 12)), x)
+    side = dot_nn(onehot((rank == i.astype(F32)) & (i < 12)), x)
+    low = dot_nn(onehot((rank == (i - 12).astype(F32)) & (i >= 12)), x)
+    high = dot_nn(onehot((rank == (i - 12 + HALF).astype(F32)) & (i >= 12)), x)
     high = pltpu.roll(high, 64, 1)
     rest = (low + high)[:, :64]
     even = jnp.concatenate([side, rest], axis=1)
@@ -250,7 +243,7 @@
         dispatch_kernel,
         out_shape=(
             jax.ShapeDtypeStruct((PAYS, 128), BF16),
-            jax.ShapeDtypeStruct((BACKS, TOK), BF16),
+            jax.ShapeDtypeStruct((TOK, BACKS), BF16),
         ),
         in_specs=[vmem(), vmem()],
         out_specs=(vmem(), vmem()),

time: 102 us -> 102 us (level)
  no operation moved by 1% of the time
where the time goes in v6:
time: 102 us
  blocking collectives  67.4 us (66%)
  starting transfers between devices  22.9 us (22%)
  Pallas kernels  6.6 us (6%)
  waiting for transfers between devices  4.57 us (4%)
    all_to_all x1, blocking collectives, local(): gathered = lax.all_to_all(blocks, ('y', 'x', 'c'), 0, 0, tiled=True)  28.3 us
    all_to_all x1, blocking collectives, local(): parts = lax.all_to_all(terms, ('y', 'x', 'c'), 0, 0, tiled=True)  22.5 us
    all_to_all x1, blocking collectives, local(): back = lax.all_to_all(shares, 'z', 0, 0, tiled=True).reshape(BACKS, 128)  16.5 us
    all_to_all x1, starting transfers between devices, local(): arrived = lax.all_to_all(payload, 'z', 0, 0, tiled=True).reshape(PAYS, 128)  15.7 us
    all_to_all x1, waiting for transfers between devices, local(): arrived = lax.all_to_all(payload, 'z', 0, 0, tiled=True).reshape(PAYS, 128)  4.56 us
    pallas_call x1, Pallas kernels, local(): pl.pallas_call(expert_kernel, out_shape=jax.ShapeDtypeStruct((2 * CHIPS,...  2.99 us
    ppermute x1, starting transfers between devices, local(): gate_b = lax.ppermute(w_gate, 'c', swap)  2.87 us
    ppermute x1, starting transfers between devices, local(): down_b = lax.ppermute(w_down, 'c', swap)  2.41 us
  transfers between devices with their start and end apart: 4, of which 1 were waited for; matrix products, arithmetic and copies ran while one was open for 0% of the time, Pallas kernels for 0%

profile of v6, /device:TPU:1, one launch (start us, length us, event | category | flops | bytes accessed | tf_op | source)
XLA Modules:
  0.0 101.6 jit_solution(10457218748324936723)
XLA Ops:
  0.0 2.1 %dispatch.1 = (bf16[320,128]{1,0:T(8,128)(2,1)}, bf16[24,288]{1,0:T(8,128)(2,1)}) custom-call(s32[2,24]{1,0:T(2,128)} %bitcast.11, bf16[24,192]{1,0:T(8,128)(2,1)} %tok_ref.1), custom_call_target="tpu_custom_call" | custom-call | tf_op jit(solution)/shard_map/dispatch/pallas_call | solution.py:242
  2.1 15.7 %all-to-all-start = ((bf16[16,10,2,128]{3,2,1,0:T(2,128)(2,1)}), bf16[16,10,2,128]{3,2,1,0:T(2,128)(2,1)S(1)}, u32[]{:S(2)}, u32[]{:S(2)}) async-start(bf16[16,10,2,128]{3,2,1,0:T(2,128)(2,1)} %bitcast.10), calls=%async_computation | async-start | bytes 163840 | tf_op jit(solution)/shard_map/all_to_all | solution.py:256
  17.8 2.9 %collective-permute-start = (bf16[6144,128]{1,0:T(8,128)(2,1)}, bf16[6144,128]{1,0:T(8,128)(2,1)S(1)}, u32[]{:S(2)}, u32[]{:S(2)}) collective-permute-start(bf16[6144,128]{1,0:T(8,128)(2,1)} %gate_a.1), channel_id=1, source_target_pairs={{0,1},{1,0},{2,3},{3,2},{4,5},{5,4},{6,7},{7,6},{8,9},{9,8},{10,11... | collective-permute-start | bytes 4718600 | tf_op jit(solution)/shard_map/ppermute | solution.py:252
  20.7 1.9 %collective-permute-start.1 = (bf16[6144,128]{1,0:T(8,128)(2,1)}, bf16[6144,128]{1,0:T(8,128)(2,1)S(1)}, u32[]{:S(2)}, u32[]{:S(2)}) collective-permute-start(bf16[6144,128]{1,0:T(8,128)(2,1)} %up_a.1), channel_id=1, source_target_pairs={{0,1},{1,0},{2,3},{3,2},{4,5},{5,4},{6,7},{7,6},{8,9},{9,8},{10,11... | collective-permute-start | bytes 4718600 | tf_op jit(solution)/shard_map/ppermute | solution.py:253
  22.6 2.4 %collective-permute-start.2 = (bf16[128,6144]{1,0:T(8,128)(2,1)}, bf16[128,6144]{1,0:T(8,128)(2,1)}, u32[]{:S(2)}, u32[]{:S(2)}) collective-permute-start(bf16[128,6144]{1,0:T(8,128)(2,1)} %down_a.1), channel_id=1, source_target_pairs={{0,1},{1,0},{2,3},{3,2},{4,5},{5,4},{6,7},{7,6},{8,9},{9,8},{10,11... | collective-permute-start | bytes 4718600 | tf_op jit(solution)/shard_map/ppermute | solution.py:254
  25.1 4.6 %all-to-all-done = bf16[16,10,2,128]{3,2,1,0:T(2,128)(2,1)S(1)} async-done(((bf16[16,10,2,128]{3,2,1,0:T(2,128)(2,1)}), bf16[16,10,2,128]{3,2,1,0:T(2,128)(2,1)S(1)}, u32[]{:S(2)}, u32[]{:S(2)}) %all-to-all-start) | async-done | bytes 81952 | tf_op jit(solution)/shard_map/all_to_all | solution.py:256
  29.6 0.0 copy-start.1
  29.6 0.0 copy-start.2
  29.6 0.3 repack.1
  30.0 0.0 copy-start
  30.0 0.0 copy-start.3
  30.0 28.3 %all_to_all.20.x_ref = bf16[32,144,128]{2,1,0:T(8,128)(2,1)S(1)} all-to-all(bf16[32,144,128]{2,1,0:T(8,128)(2,1)S(1)} %get-tuple-element.11), channel_id=1, replica_groups=mesh['z'=16,'y'=4,'x'=4,'c'=2] {'y','x','c'}, dimensions={0} | all-to-all | bytes 2359296 | tf_op jit(solution)/shard_map/all_to_all | solution.py:269
  58.3 0.0 collective-permute-done.gate_b
  58.3 0.0 collective-permute-done.1.up_b
  58.3 0.0 collective-permute-done.2.down_b
  58.3 0.0 copy-done.1
  58.3 0.0 copy-done.2
  58.3 0.0 copy-done
  58.4 0.0 copy-done.3
  58.4 3.0 %expert.1 = bf16[32,144,128]{2,1,0:T(8,128)(2,1)S(1)} custom-call(bf16[32,144,128]{2,1,0:T(8,128)(2,1)S(1)} %all_to_all.20.x_ref, f32[96,128]{1,0:T(8,128)S(1)} %get-tuple-element.12.info_ref, bf16[8,6144]{1,0:T(8,128)(2,1)S(1)} %bitcast.8, bf16[6144,128]{1,0:T(8,128)(2,1)S(1)} %copy-done, bf16[6144,128]{1,0:T(8,128)(2,1)S(1)} %collective-permute-done.gate_b, ...), custom_call_target="tpu_custom_call" | custom-call | tf_op jit(solution)/shard_map/expert/pallas_call | solution.py:270
  61.4 0.0 copy-start.4
  61.4 22.5 %all_to_all.21.in_ref = bf16[32,144,128]{2,1,0:T(8,128)(2,1)S(1)} all-to-all(bf16[32,144,128]{2,1,0:T(8,128)(2,1)S(1)} %expert.1), channel_id=1, replica_groups=mesh['z'=16,'y'=4,'x'=4,'c'=2] {'y','x','c'}, dimensions={0} | all-to-all | bytes 2359296 | tf_op jit(solution)/shard_map/all_to_all | solution.py:282
  83.9 0.4 share.1
  84.3 16.5 %all_to_all.22 = bf16[16,9,2,128]{3,2,1,0:T(2,128)(2,1)S(1)} all-to-all(bf16[16,9,2,128]{3,2,1,0:T(2,128)(2,1)S(1)} %bitcast.6), channel_id=1, replica_groups=mesh['z'=16,'y'=4,'x'=4,'c'=2] {'z'}, dimensions={0} | all-to-all | bytes 147456 | tf_op jit(solution)/shard_map/all_to_all | solution.py:292
  100.8 0.0 copy-done.4
  100.8 0.8 combine.1
Async XLA Ops:
  2.1 27.5 %all-to-all-start = ((bf16[16,10,2,128]{3,2,1,0:T(2,128)(2,1)}), bf16[16,10,2,128]{3,2,1,0:T(2,128)(2,1)S(1)}, u32[]{:S(2)}, u32[]{:S(2)}) async-start(bf16[16,10,2,128]{3,2,1,0:T(2,128)(2,1)} %bitcast.10), calls=%async_computation | async-start | bytes 163840 | tf_op jit(solution)/shard_map/all_to_all | solution.py:256
  17.8 40.5 %collective-permute-start = (bf16[6144,128]{1,0:T(8,128)(2,1)}, bf16[6144,128]{1,0:T(8,128)(2,1)S(1)}, u32[]{:S(2)}, u32[]{:S(2)}) collective-permute-start(bf16[6144,128]{1,0:T(8,128)(2,1)} %gate_a.1), channel_id=1, source_target_pairs={{0,1},{1,0},{2,3},{3,2},{4,5},{5,4},{6,7},{7,6},{8,9},{9,8},{10,11... | collective-permute-start | bytes 4718600 | tf_op jit(solution)/shard_map/ppermute | solution.py:252
  20.7 37.6 %collective-permute-start.1 = (bf16[6144,128]{1,0:T(8,128)(2,1)}, bf16[6144,128]{1,0:T(8,128)(2,1)S(1)}, u32[]{:S(2)}, u32[]{:S(2)}) collective-permute-start(bf16[6144,128]{1,0:T(8,128)(2,1)} %up_a.1), channel_id=1, source_target_pairs={{0,1},{1,0},{2,3},{3,2},{4,5},{5,4},{6,7},{7,6},{8,9},{9,8},{10,11... | collective-permute-start | bytes 4718600 | tf_op jit(solution)/shard_map/ppermute | solution.py:253
  22.6 35.7 %collective-permute-start.2 = (bf16[128,6144]{1,0:T(8,128)(2,1)}, bf16[128,6144]{1,0:T(8,128)(2,1)}, u32[]{:S(2)}, u32[]{:S(2)}) collective-permute-start(bf16[128,6144]{1,0:T(8,128)(2,1)} %down_a.1), channel_id=1, source_target_pairs={{0,1},{1,0},{2,3},{3,2},{4,5},{5,4},{6,7},{7,6},{8,9},{9,8},{10,11... | collective-permute-start | bytes 4718600 | tf_op jit(solution)/shard_map/ppermute | solution.py:254
  29.6 28.7 %copy-start.1 = (bf16[6144,128]{1,0:T(8,128)(2,1)S(1)}, bf16[6144,128]{1,0:T(8,128)(2,1)}, u32[]{:S(2)}) copy-start(bf16[6144,128]{1,0:T(8,128)(2,1)} %up_a.1) | copy-start | bytes 4718596
  29.6 28.7 %copy-start.2 = (bf16[128,6144]{1,0:T(8,128)(2,1)S(1)}, bf16[128,6144]{1,0:T(8,128)(2,1)}, u32[]{:S(2)}) copy-start(bf16[128,6144]{1,0:T(8,128)(2,1)} %down_a.1) | copy-start | bytes 4718596
  30.0 28.4 %copy-start = (bf16[6144,128]{1,0:T(8,128)(2,1)S(1)}, bf16[6144,128]{1,0:T(8,128)(2,1)}, u32[]{:S(2)}) copy-start(bf16[6144,128]{1,0:T(8,128)(2,1)} %gate_a.1) | copy-start | bytes 4718596
  30.0 28.4 %copy-start.3 = (bf16[6144,8]{0,1:T(8,128)(2,1)S(1)}, bf16[6144,8]{0,1:T(8,128)(2,1)}, u32[]{:S(2)}) copy-start(bf16[6144,8]{0,1:T(8,128)(2,1)} %param.8) | copy-start | bytes 294916
  61.4 39.4 %copy-start.4 = (bf16[24,288]{1,0:T(8,128)(2,1)S(1)}, bf16[24,288]{1,0:T(8,128)(2,1)}, u32[]{:S(2)}) copy-start(bf16[24,288]{1,0:T(8,128)(2,1)} %get-tuple-element.9.rank_ref) | copy-start | bytes 41476

commit v7 on v6

--- a/solution.py
+++ b/solution.py
@@ -97,7 +97,9 @@
     named = onehot((k8 == first) | (k8 == second))
     lane = iota((EXPERTS, 128), 1)
     named_lane = dot_tn(named, onehot((lane & 7) == iota((EXPERTS, 128), 0)))
-    rank_col = dot_tn(rank, onehot(iota((EXPERTS, EXPERTS), 0) == iota((EXPERTS, EXPERTS), 1)))
+    same = onehot(iota((EXPERTS, EXPERTS), 0) == iota((EXPERTS, EXPERTS), 1))
+    count_col = dot_nt(onehot(iota((TOK, TOK), 1) < iota((TOK, TOK), 0)), named)
+    rank_col = jnp.where(dot_tn(named, same) > 0.5, count_col, 100.0)
     slot = (iota((TOK, 128), 1) >> 3).astype(F32)
     marks = [
         jnp.sum(jnp.where(rank_col[:, k : k + 1] == slot, named_lane, 0.0), axis=0, keepdims=True)

time: 102 us -> 102 us (level)
  no operation moved by 1% of the time
where the time goes in v7:
time: 102 us
  blocking collectives  67.4 us (66%)
  starting transfers between devices  22.9 us (22%)
  Pallas kernels  6.61 us (6%)
  waiting for transfers between devices  4.57 us (4%)
    all_to_all x1, blocking collectives, local(): gathered = lax.all_to_all(blocks, ('y', 'x', 'c'), 0, 0, tiled=True)  28.4 us
    all_to_all x1, blocking collectives, local(): parts = lax.all_to_all(terms, ('y', 'x', 'c'), 0, 0, tiled=True)  22.5 us
    all_to_all x1, blocking collectives, local(): back = lax.all_to_all(shares, 'z', 0, 0, tiled=True).reshape(BACKS, 128)  16.5 us
    all_to_all x1, starting transfers between devices, local(): arrived = lax.all_to_all(payload, 'z', 0, 0, tiled=True).reshape(PAYS, 128)  15.7 us
    all_to_all x1, waiting for transfers between devices, local(): arrived = lax.all_to_all(payload, 'z', 0, 0, tiled=True).reshape(PAYS, 128)  4.56 us
    pallas_call x1, Pallas kernels, local(): pl.pallas_call(expert_kernel, out_shape=jax.ShapeDtypeStruct((2 * CHIPS,...  3 us
    ppermute x1, starting transfers between devices, local(): gate_b = lax.ppermute(w_gate, 'c', swap)  2.87 us
    ppermute x1, starting transfers between devices, local(): down_b = lax.ppermute(w_down, 'c', swap)  2.41 us
  transfers between devices with their start and end apart: 4, of which 1 were waited for; matrix products, arithmetic and copies ran while one was open for 0% of the time, Pallas kernels for 0%

profile of v7, /device:TPU:1, one launch (start us, length us, event | category | flops | bytes accessed | tf_op | source)
XLA Modules:
  0.0 101.6 jit_solution(17973570843618514665)
XLA Ops:
  0.0 2.1 %dispatch.1 = (bf16[320,128]{1,0:T(8,128)(2,1)}, bf16[24,288]{1,0:T(8,128)(2,1)}) custom-call(s32[2,24]{1,0:T(2,128)} %bitcast.11, bf16[24,192]{1,0:T(8,128)(2,1)} %tok_ref.1), custom_call_target="tpu_custom_call" | custom-call | tf_op jit(solution)/shard_map/dispatch/pallas_call | solution.py:244
  2.1 15.7 %all-to-all-start = ((bf16[16,10,2,128]{3,2,1,0:T(2,128)(2,1)}), bf16[16,10,2,128]{3,2,1,0:T(2,128)(2,1)S(1)}, u32[]{:S(2)}, u32[]{:S(2)}) async-start(bf16[16,10,2,128]{3,2,1,0:T(2,128)(2,1)} %bitcast.10), calls=%async_computation | async-start | bytes 163840 | tf_op jit(solution)/shard_map/all_to_all | solution.py:258
  17.8 2.9 %collective-permute-start = (bf16[6144,128]{1,0:T(8,128)(2,1)}, bf16[6144,128]{1,0:T(8,128)(2,1)S(1)}, u32[]{:S(2)}, u32[]{:S(2)}) collective-permute-start(bf16[6144,128]{1,0:T(8,128)(2,1)} %gate_a.1), channel_id=1, source_target_pairs={{0,1},{1,0},{2,3},{3,2},{4,5},{5,4},{6,7},{7,6},{8,9},{9,8},{10,11... | collective-permute-start | bytes 4718600 | tf_op jit(solution)/shard_map/ppermute | solution.py:254
  20.7 1.9 %collective-permute-start.1 = (bf16[6144,128]{1,0:T(8,128)(2,1)}, bf16[6144,128]{1,0:T(8,128)(2,1)S(1)}, u32[]{:S(2)}, u32[]{:S(2)}) collective-permute-start(bf16[6144,128]{1,0:T(8,128)(2,1)} %up_a.1), channel_id=1, source_target_pairs={{0,1},{1,0},{2,3},{3,2},{4,5},{5,4},{6,7},{7,6},{8,9},{9,8},{10,11... | collective-permute-start | bytes 4718600 | tf_op jit(solution)/shard_map/ppermute | solution.py:255
  22.6 2.4 %collective-permute-start.2 = (bf16[128,6144]{1,0:T(8,128)(2,1)}, bf16[128,6144]{1,0:T(8,128)(2,1)}, u32[]{:S(2)}, u32[]{:S(2)}) collective-permute-start(bf16[128,6144]{1,0:T(8,128)(2,1)} %down_a.1), channel_id=1, source_target_pairs={{0,1},{1,0},{2,3},{3,2},{4,5},{5,4},{6,7},{7,6},{8,9},{9,8},{10,11... | collective-permute-start | bytes 4718600 | tf_op jit(solution)/shard_map/ppermute | solution.py:256
  25.1 4.6 %all-to-all-done = bf16[16,10,2,128]{3,2,1,0:T(2,128)(2,1)S(1)} async-done(((bf16[16,10,2,128]{3,2,1,0:T(2,128)(2,1)}), bf16[16,10,2,128]{3,2,1,0:T(2,128)(2,1)S(1)}, u32[]{:S(2)}, u32[]{:S(2)}) %all-to-all-start) | async-done | bytes 81952 | tf_op jit(solution)/shard_map/all_to_all | solution.py:258
  29.6 0.0 copy-start.1
  29.6 0.0 copy-start.2
  29.6 0.3 repack.1
  30.0 0.0 copy-start
  30.0 0.0 copy-start.3
  30.0 28.4 %all_to_all.20.x_ref = bf16[32,144,128]{2,1,0:T(8,128)(2,1)S(1)} all-to-all(bf16[32,144,128]{2,1,0:T(8,128)(2,1)S(1)} %get-tuple-element.11), channel_id=1, replica_groups=mesh['z'=16,'y'=4,'x'=4,'c'=2] {'y','x','c'}, dimensions={0} | all-to-all | bytes 2359296 | tf_op jit(solution)/shard_map/all_to_all | solution.py:271
  58.4 0.0 collective-permute-done.gate_b
  58.4 0.0 collective-permute-done.1.up_b
  58.4 0.0 collective-permute-done.2.down_b
  58.4 0.0 copy-done.1
  58.4 0.0 copy-done.2
  58.4 0.0 copy-done
  58.4 0.0 copy-done.3
  58.4 3.0 %expert.1 = bf16[32,144,128]{2,1,0:T(8,128)(2,1)S(1)} custom-call(bf16[32,144,128]{2,1,0:T(8,128)(2,1)S(1)} %all_to_all.20.x_ref, f32[96,128]{1,0:T(8,128)S(1)} %get-tuple-element.12.info_ref, bf16[8,6144]{1,0:T(8,128)(2,1)S(1)} %bitcast.8, bf16[6144,128]{1,0:T(8,128)(2,1)S(1)} %copy-done, bf16[6144,128]{1,0:T(8,128)(2,1)S(1)} %collective-permute-done.gate_b, ...), custom_call_target="tpu_custom_call" | custom-call | tf_op jit(solution)/shard_map/expert/pallas_call | solution.py:272
  61.4 0.0 copy-start.4
  61.4 22.5 %all_to_all.21.in_ref = bf16[32,144,128]{2,1,0:T(8,128)(2,1)S(1)} all-to-all(bf16[32,144,128]{2,1,0:T(8,128)(2,1)S(1)} %expert.1), channel_id=1, replica_groups=mesh['z'=16,'y'=4,'x'=4,'c'=2] {'y','x','c'}, dimensions={0} | all-to-all | bytes 2359296 | tf_op jit(solution)/shard_map/all_to_all | solution.py:284
  84.0 0.4 share.1
  84.3 16.5 %all_to_all.22 = bf16[16,9,2,128]{3,2,1,0:T(2,128)(2,1)S(1)} all-to-all(bf16[16,9,2,128]{3,2,1,0:T(2,128)(2,1)S(1)} %bitcast.6), channel_id=1, replica_groups=mesh['z'=16,'y'=4,'x'=4,'c'=2] {'z'}, dimensions={0} | all-to-all | bytes 147456 | tf_op jit(solution)/shard_map/all_to_all | solution.py:294
  100.8 0.0 copy-done.4
  100.8 0.8 combine.1
Async XLA Ops:
  2.1 27.5 %all-to-all-start = ((bf16[16,10,2,128]{3,2,1,0:T(2,128)(2,1)}), bf16[16,10,2,128]{3,2,1,0:T(2,128)(2,1)S(1)}, u32[]{:S(2)}, u32[]{:S(2)}) async-start(bf16[16,10,2,128]{3,2,1,0:T(2,128)(2,1)} %bitcast.10), calls=%async_computation | async-start | bytes 163840 | tf_op jit(solution)/shard_map/all_to_all | solution.py:258
  17.8 40.5 %collective-permute-start = (bf16[6144,128]{1,0:T(8,128)(2,1)}, bf16[6144,128]{1,0:T(8,128)(2,1)S(1)}, u32[]{:S(2)}, u32[]{:S(2)}) collective-permute-start(bf16[6144,128]{1,0:T(8,128)(2,1)} %gate_a.1), channel_id=1, source_target_pairs={{0,1},{1,0},{2,3},{3,2},{4,5},{5,4},{6,7},{7,6},{8,9},{9,8},{10,11... | collective-permute-start | bytes 4718600 | tf_op jit(solution)/shard_map/ppermute | solution.py:254
  20.7 37.7 %collective-permute-start.1 = (bf16[6144,128]{1,0:T(8,128)(2,1)}, bf16[6144,128]{1,0:T(8,128)(2,1)S(1)}, u32[]{:S(2)}, u32[]{:S(2)}) collective-permute-start(bf16[6144,128]{1,0:T(8,128)(2,1)} %up_a.1), channel_id=1, source_target_pairs={{0,1},{1,0},{2,3},{3,2},{4,5},{5,4},{6,7},{7,6},{8,9},{9,8},{10,11... | collective-permute-start | bytes 4718600 | tf_op jit(solution)/shard_map/ppermute | solution.py:255
  22.6 35.7 %collective-permute-start.2 = (bf16[128,6144]{1,0:T(8,128)(2,1)}, bf16[128,6144]{1,0:T(8,128)(2,1)}, u32[]{:S(2)}, u32[]{:S(2)}) collective-permute-start(bf16[128,6144]{1,0:T(8,128)(2,1)} %down_a.1), channel_id=1, source_target_pairs={{0,1},{1,0},{2,3},{3,2},{4,5},{5,4},{6,7},{7,6},{8,9},{9,8},{10,11... | collective-permute-start | bytes 4718600 | tf_op jit(solution)/shard_map/ppermute | solution.py:256
  29.6 28.8 %copy-start.1 = (bf16[6144,128]{1,0:T(8,128)(2,1)S(1)}, bf16[6144,128]{1,0:T(8,128)(2,1)}, u32[]{:S(2)}) copy-start(bf16[6144,128]{1,0:T(8,128)(2,1)} %up_a.1) | copy-start | bytes 4718596
  29.6 28.8 %copy-start.2 = (bf16[128,6144]{1,0:T(8,128)(2,1)S(1)}, bf16[128,6144]{1,0:T(8,128)(2,1)}, u32[]{:S(2)}) copy-start(bf16[128,6144]{1,0:T(8,128)(2,1)} %down_a.1) | copy-start | bytes 4718596
  30.0 28.4 %copy-start = (bf16[6144,128]{1,0:T(8,128)(2,1)S(1)}, bf16[6144,128]{1,0:T(8,128)(2,1)}, u32[]{:S(2)}) copy-start(bf16[6144,128]{1,0:T(8,128)(2,1)} %gate_a.1) | copy-start | bytes 4718596
  30.0 28.4 %copy-start.3 = (bf16[6144,8]{0,1:T(8,128)(2,1)S(1)}, bf16[6144,8]{0,1:T(8,128)(2,1)}, u32[]{:S(2)}) copy-start(bf16[6144,8]{0,1:T(8,128)(2,1)} %param.8) | copy-start | bytes 294916
  61.4 39.4 %copy-start.4 = (bf16[24,288]{1,0:T(8,128)(2,1)S(1)}, bf16[24,288]{1,0:T(8,128)(2,1)}, u32[]{:S(2)}) copy-start(bf16[24,288]{1,0:T(8,128)(2,1)} %get-tuple-element.9.rank_ref) | copy-start | bytes 41476
